TPU v7x, 32 devices: a whole 2x2x4 slice. The times are simulated.
32 devices in a mesh: dp: 8 (over z, y), tensor: 4 (over x, core).
Axes of the slice: x: 2, y: 2, z: 4, core: 2. Of those that a mesh axis runs over, the one named last changes fastest.
Arguments:
- tokens: bfloat16 [8, 1024, 2048], P('dp'), may hold values from -6 to 6
- segment_ids: int32 [8, 1024], P('dp'), may hold values from 0 to 7, never falling along the last dimension, each value on 1 to 512 neighbouring positions
- out_grad: bfloat16 [8, 1024, 2048], P('dp'), may hold values from -6 to 6
- attn_norm_gain: float32 [2048], replicated, may hold values from 0.5 to 1.5
- attn_norm_bias: float32 [2048], replicated, may hold values from -1.75 to 1.75
- mlp_norm_gain: float32 [2048], replicated, may hold values from 0.5 to 1.5
- mlp_norm_bias: float32 [2048], replicated, may hold values from -1.75 to 1.75
- qkv_weight: float32 [2048, 8, 3, 256], P('dp', 'tensor'), may hold values from -0.1875 to 0.1875
- qv_bias: float32 [8, 2, 256], P('tensor'), may hold values from -1.75 to 1.75
- key_bias: float32 [8, 64], P('tensor'), may hold values from -3 to 3
- dense_weight: float32 [8, 256, 2048], P('tensor', None, 'dp'), may hold values from -0.75 to 0.75
- dense_bias: float32 [2048], replicated, may hold values from -1.75 to 1.75
- up_weight: float32 [2048, 8192], P('dp', 'tensor'), may hold values from -0.125 to 0.125
- up_bias: float32 [8192], P('tensor'), may hold values from -3 to 3
- down_weight: float32 [8192, 2048], P('tensor', 'dp'), may hold values from -0.0625 to 0.0625
- down_bias: float32 [2048], replicated, may hold values from -1.75 to 1.75
Outputs:
- block_out: bfloat16 [8, 1024, 2048], P('dp')
- input_grad: bfloat16 [8, 1024, 2048], P('dp')
- attn_norm_gain_grad: float32 [2048], replicated
- attn_norm_bias_grad: float32 [2048], replicated
- mlp_norm_gain_grad: float32 [2048], replicated
- mlp_norm_bias_grad: float32 [2048], replicated
- qkv_weight_grad: float32 [2048, 8, 3, 256], P('dp', 'tensor')
- qv_bias_grad: float32 [8, 2, 256], P('tensor')
- key_bias_grad: float32 [8, 64], P('tensor')
- dense_weight_grad: float32 [8, 256, 2048], P('tensor', None, 'dp')
- dense_bias_grad: float32 [2048], replicated
- up_weight_grad: float32 [2048, 8192], P('dp', 'tensor')
- up_bias_grad: float32 [8192], P('tensor')
- down_weight_grad: float32 [8192, 2048], P('tensor', 'dp')
- down_bias_grad: float32 [2048], replicated
Inputs may be any that keep to these rules, and one draw needn't show every extreme that they name: `segment_ids`: ids never fall along a sequence; each of the 8 documents of a sequence holds 1 to 512 tokens, one exactly 512.
All inputs are finite; a program needn't handle non-finite values.
Results may differ from a plain program's by a relative error of at most 0.007.
The roundings to bfloat16 on the way count: a program that leaves them out, or rounds other values in their place, can miss the bound.
Values may be sent and summed in bfloat16 or wider, within the bound.
A program may use at most 256 MiB of HBM per device.

v0:
```python
import functools

import jax
import jax.numpy as jnp
from jax import lax
from jax.experimental import pallas as pl
from jax.experimental.pallas import tpu as pltpu
from jax.sharding import PartitionSpec as P

ROT = 64
PAIR = 2
QBLOCK = 256
DOC_MAX = 512
F = jnp.float32
B = jnp.bfloat16


def dot(left, right, dims, kind):
    return lax.dot_general(left, right, (dims, ((), ())), preferred_element_type=F).astype(kind)


def gelu_slope(pre_act):
    cumulative = 0.5 * (1.0 + lax.erf(pre_act * 0.7071067811865476))
    density = jnp.exp(-0.5 * pre_act * pre_act) * 0.3989422804014327
    return cumulative + pre_act * density


def rope_tables(length):
    half = ROT // 2
    frequency = 10000.0 ** (-(jnp.arange(half, dtype=F) * 2.0) / ROT)
    angles = jnp.arange(length, dtype=F)[:, None] * frequency[None, :]
    cosine, sine = jnp.cos(angles), jnp.sin(angles)
    flat = jnp.zeros((length, 128 - ROT), F)
    zero = jnp.zeros_like(sine)
    return (
        jnp.concatenate([cosine, cosine, flat + 1.0], axis=1),
        jnp.concatenate([-sine, zero, flat], axis=1),
        jnp.concatenate([zero, sine, flat], axis=1),
    )


def turn(rows, cosine, from_above, from_below):
    head = rows[:, :128]
    above = pltpu.roll(head, 128 - ROT // 2, 1)
    below = pltpu.roll(head, ROT // 2, 1)
    turned = head * cosine + above * from_above + below * from_below
    return jnp.concatenate([turned, rows[:, 128:]], axis=1)


def block_mask(seg_col_ref, seg_row_ref, first, low, high):
    rows = first + lax.broadcasted_iota(jnp.int32, (QBLOCK, high - low), 0)
    columns = low + lax.broadcasted_iota(jnp.int32, (QBLOCK, high - low), 1)
    same = seg_col_ref[0, first : first + QBLOCK, :] == seg_row_ref[0, :, low:high]
    return (columns <= rows) & same


def key_range(first):
    return max(0, first - DOC_MAX), first + QBLOCK


def attn_forward(mixed_ref, bias_ref, cos_ref, up_ref, down_ref, col_ref, row_ref, q_ref, k_ref, v_ref, ctx_ref, lse_ref):
    size = q_ref.shape[2]
    length = q_ref.shape[1]
    scale = size ** (-0.5)
    tables = (cos_ref[...], up_ref[...], down_ref[...])
    q_ref[0] = turn(mixed_ref[0, :, :size] + bias_ref[:, :size], *tables).astype(B)
    k_ref[0] = turn(mixed_ref[0, :, size : 2 * size] + bias_ref[:, size : 2 * size], *tables).astype(B)
    v_ref[0] = (mixed_ref[0, :, 2 * size :] + bias_ref[:, 2 * size :]).astype(B)
    for first in range(0, length, QBLOCK):
        low, high = key_range(first)
        scores = dot(q_ref[0, first : first + QBLOCK], k_ref[0, low:high], ((1,), (1,)), F) * scale
        scores = jnp.where(block_mask(col_ref, row_ref, first, low, high), scores, -1e30)
        row_max = jnp.max(scores, axis=1, keepdims=True)
        expo = jnp.exp(scores - row_max)
        total = jnp.sum(expo, axis=1, keepdims=True)
        probs = (expo / total).astype(B)
        ctx_ref[0, first : first + QBLOCK] = dot(probs, v_ref[0, low:high], ((1,), (0,)), B)
        lse_ref[0, first : first + QBLOCK] = row_max + jnp.log(total)


def attn_backward(q_ref, k_ref, v_ref, grad_ref, lse_ref, cos_ref, up_ref, down_ref, col_ref, row_ref, mixed_ref, sum_ref, q_acc, k_acc, v_acc):
    size = q_ref.shape[2]
    length = q_ref.shape[1]
    scale = size ** (-0.5)
    k_acc[...] = jnp.zeros_like(k_acc)
    v_acc[...] = jnp.zeros_like(v_acc)
    for first in range(0, length, QBLOCK):
        low, high = key_range(first)
        here = slice(first, first + QBLOCK)
        scores = dot(q_ref[0, here], k_ref[0, low:high], ((1,), (1,)), F) * scale
        scores = jnp.where(block_mask(col_ref, row_ref, first, low, high), scores, -1e30)
        probs = jnp.exp(scores - lse_ref[0, here])
        v_acc[low:high] += dot(probs.astype(B), grad_ref[0, here], ((0,), (0,)), F)
        prob_grad = dot(grad_ref[0, here], v_ref[0, low:high], ((1,), (1,)), F)
        centred = jnp.sum(probs * prob_grad, axis=1, keepdims=True)
        score_grad = (probs * (prob_grad - centred)).astype(B)
        q_acc[here] = dot(score_grad, k_ref[0, low:high], ((1,), (0,)), F) * scale
        k_acc[low:high] += dot(score_grad, q_ref[0, here], ((0,), (0,)), F) * scale
    tables = (cos_ref[...], -up_ref[...], -down_ref[...])
    q_grad = turn(q_acc[...], *tables).astype(B)
    k_grad = turn(k_acc[...], *tables).astype(B)
    v_grad = v_acc[...].astype(B)
    for number, part in enumerate((q_grad, k_grad, v_grad)):
        mixed_ref[0, :, number * size : (number + 1) * size] = part
        sum_ref[0, :, number * size : (number + 1) * size] = jnp.sum(part.astype(F), axis=0, keepdims=True)


def per_seq(rows, columns):
    return pl.BlockSpec((1, rows, columns), lambda seq, *_: (seq, 0, 0))


def shared(rows, columns):
    return pl.BlockSpec((rows, columns), lambda *_: (0, 0))


MESH = pl.DeviceIdType.MESH
CHUNK = 256


def bit_of(index, bit):
    return lax.rem(lax.div(index, bit), 2)


def flip(index, mask):
    bit = 1
    while bit <= mask:
        if mask & bit:
            index = index + bit * (1 - 2 * bit_of(index, bit))
        bit *= 2
    return index


def block_order(groups):
    spread = [bit for bit in (1 << k for k in reversed(range(groups.bit_length() - 1))) if bit != PAIR]
    order = [0, PAIR]
    for bit in spread:
        order = order + [mask | bit for mask in order]
    return spread, order


def stats(rows):
    mean = jnp.mean(rows, axis=1, keepdims=True)
    center = rows - mean
    return mean, lax.rsqrt(jnp.mean(center * center, axis=1, keepdims=True) + 1e-05)


def greet(partners):
    barrier = pltpu.get_barrier_semaphore()
    for axis, index in partners:
        pl.semaphore_signal(barrier, inc=1, device_id={axis: index}, device_id_type=MESH)
    pl.semaphore_wait(barrier, len(partners))


GATHERING = (
    ("x1", "i"),
    ("sh", 0, 1),
    ("pu", 0, "i"),
    ("pu", 0, "o"),
    ("sh", 2, 0),
    ("sh", 0, 0),
    ("hd", 0, "o"),
    ("yo", 2, 0),
    ("yo", 0, 0),
    ("hd", 0, "i"),
    ("st", 0),
    ("x1", "o"),
    ("sh", 1, 1),
    ("sh", 1, 0),
    ("sh", 2, 1),
    ("po", 0, 0),
    ("pu", 1, "o"),
    ("N", 0),
    ("re", 0),
    ("pu", 1, "i"),
    ("hd", 1, "i"),
    ("yo", 1, 0),
    ("yo", 0, 1),
    ("st", 1),
    ("hd", 1, "o"),
    ("po", 0, 1),
    ("g1", "o"),
    ("G", 0),
    ("x2",),
    ("yo", 0, 2),
    ("yo", 0, 3),
    ("po", 0, 2),
    ("g1", "i"),
    ("po", 1, 1),
    ("po", 1, 0),
    ("pu", 2, "o"),
    ("PJ", 0),
    ("re", 1),
    ("CG", 0),
    ("hd", 2, "o"),
    ("pu", 2, "i"),
    ("hd", 2, "i"),
    ("yo", 1, 1),
    ("AT", 0),
    ("g2",),
    ("GR", 0, 0),
    ("po", 1, 2),
    ("x3",),
    ("yo", 1, 2),
    ("GR", 0, 1),
    ("N", 1),
    ("yo", 2, 1),
    ("re", 2),
    ("po", 2, 1),
    ("PJ", 1),
    ("po", 2, 0),
    ("g3",),
    ("yo", 1, 3),
    ("G", 1),
    ("CG", 1),
    ("st", 2),
    ("AT", 1),
    ("yo", 2, 2),
    ("po", 2, 2),
    ("GR", 1, 0),
    ("UP", 0),
    ("yo", 2, 3),
    ("UP", 1),
    ("GR", 1, 1),
)


def gather_kernel(
    groups,
    qkv_ref,
    dense_ref,
    up_ref,
    down_ref,
    seg_ref,
    x_ref,
    g_ref,
    vec_ref,
    up_bias_ref,
    offset_ref,
    cos_ref,
    above_ref,
    below_ref,
    w_out,
    w_relay,
    x_other,
    g_other,
    x_rel,
    g_rel,
    mlp_out,
    mixed_out,
    ctx_out,
    act_out,
    slope_out,
    send_out,
    keep_out,
    sum_ref,
    bias_ref,
    w,
    raw_x,
    raw_g,
    attn_v,
    g_v,
    mlp_v,
    xr_v,
    grad_v,
    send_v,
    q_v,
    k_v,
    v_v,
    cg_v,
    ctx_v,
    mg_v,
    dk_v,
    dv_v,
    act_v,
    slope_v,
    theirs_v,
    seg_v,
    col_v,
    send_sem,
    recv_sem,
    cross_sem,
    two_sem,
    three_sem,
    relay_sem,
    quarter_sem,
    shard_sem,
    seg_sem,
    load_sem,
    rel_sem,
    tile_sem,
    out_sem,
):
    length, width = x_ref.shape
    part = width // groups
    size = q_v.shape[1]
    quarter = length // 4
    me, place = lax.axis_index("dp"), lax.axis_index("tensor")
    core, side = lax.rem(place, 2), lax.div(place, 2)
    pair_to, side_to, core_to = flip(me, PAIR), flip(place, 2), flip(place, 1)
    spread, order = block_order(groups)
    half = bit_of(me, PAIR)
    hidden = slope_v.shape[2]

    def shards(owner, slot):
        at = pl.ds(pl.multiple_of(owner * 3 * size, 128), 3 * size)
        spots = [
            (qkv_ref.at[:, at], grad_v.at[pl.ds(slot * part, part), pl.ds(0, 3 * size)]),
            (dense_ref.at[owner], grad_v.at[pl.ds(2 * part, size), pl.ds(slot * part, part)]),
            (
                up_ref.at[:, pl.ds(pl.multiple_of(owner * hidden, hidden), hidden)],
                grad_v.at[pl.ds((3 + slot) * part, part)],
            ),
        ]
        for number in range(hidden // part):
            at = pl.ds(pl.multiple_of(owner * hidden + number * part, part), part)
            spots.append((down_ref.at[at], slope_v.at[slot, :, pl.ds(number * part, part)]))
        return [
            pltpu.make_async_copy(source, target, shard_sem.at[slot, number])
            for number, (source, target) in enumerate(spots)
        ]

    shard_copies = [shards(half, 0), shards(1 - half, 1)]
    for number in range(3 + hidden // part):
        for slot in (1, 0):
            shard_copies[slot][number].start()

    def shard(group, slot):
        for copy in shard_copies[slot][(0, 2, 3)[group] : (2, 3, None)[group]]:
            copy.wait()

        def put(columns, value):
            if slot:
                theirs_v[group, :, columns] = value.astype(B)
            else:
                w[group, 0:part, columns] = value.astype(B)

        if group == 0:
            put(slice(0, 3 * size), grad_v[slot * part : (slot + 1) * part, : 3 * size])
            put(slice(3 * size, 4 * size), grad_v[2 * part : 2 * part + size, slot * part : (slot + 1) * part].T)
        elif group == 1:
            put(slice(0, hidden), grad_v[(3 + slot) * part : (4 + slot) * part])
        else:
            for number in range(hidden // part):
                at = slice(number * part, (number + 1) * part)
                put(at, slope_v[slot, :, at].T)

    across = PAIR | spread[0]
    inner = bit_of(me, PAIR) != bit_of(me, spread[0])
    greet(
        [("dp", flip(me, mask)) for mask in [PAIR, across] + spread] + [("tensor", side_to), ("tensor", core_to)]
    )
    outer = bit_of(me, PAIR) == bit_of(me, spread[0])
    copies, partial_copies = {}, []

    def remote(key, source, target, axis, index):
        number = len(copies)
        copies[key] = pltpu.make_async_remote_copy(
            src_ref=source,
            dst_ref=target,
            send_sem=send_sem.at[number],
            recv_sem=recv_sem.at[number],
            device_id={axis: index},
            device_id_type=MESH,
        )
        copies[key].start()

    def rows(position):
        return pl.ds(position * part, part)

    def pair_up(group, here=None):
        key = ("w", group, 1)
        if key not in copies:
            number = len(copies)
            copies[key] = pltpu.make_async_remote_copy(
                src_ref=theirs_v.at[group],
                dst_ref=w.at[group, rows(1)],
                send_sem=send_sem.at[number],
                recv_sem=recv_sem.at[number],
                device_id={"dp": pair_to},
                device_id_type=MESH,
            )
        if here is None:
            copies[key].start()
        else:
            pl.when(here)(copies[key].start)

    def onward(group, position, level):
        source = w.at[group, rows(position)]
        far = position + (2 << level)
        remote(("w", group, far), source, w.at[group, rows(far)], "dp", flip(me, spread[level]))

    def partly(here, source, target, send, recv, to):
        copy = pltpu.make_async_remote_copy(
            src_ref=source,
            dst_ref=target,
            send_sem=send,
            recv_sem=recv,
            device_id={"dp": to},
            device_id_type=MESH,
        )
        partial_copies.append((here, copy))
        pl.when(here)(copy.start)
        return copy

    across_to = flip(me, across)

    def straight(group):
        copy = partly(
            inner, theirs_v.at[group], w.at[group, rows(3)], cross_sem.at[group, 0], three_sem.at[group], across_to
        )
        copies[("w", group, 3)] = copy

    def hand(group, here=None):
        source, sem = w.at[group, rows(0)], cross_sem.at[group, 1]
        if here is not inner:
            partly(outer, source, w_relay.at[group, rows(0)], sem, relay_sem.at[group, 0], pair_to)
        if here is not outer:
            partly(inner, source, w_relay.at[group, rows(1)], sem, relay_sem.at[group, 1], across_to)

    def relay(group):
        source = w.at[group, rows(1)]
        partly(
            inner, source, w_relay.at[group, rows(2)], cross_sem.at[group, 2], relay_sem.at[group, 2], across_to
        )

    def pass_on(group, *numbers):
        for number in numbers:
            source, target = w_relay.at[group, rows(number)], 3 if number == 2 else 2
            here = pltpu.make_async_remote_copy(
                src_ref=source,
                dst_ref=source,
                send_sem=relay_sem.at[group, number],
                recv_sem=relay_sem.at[group, number],
                device_id={"dp": pair_to},
                device_id_type=MESH,
            )
            pl.when(inner)(here.wait_recv)
            copy = partly(
                inner,
                source,
                w.at[group, rows(target)],
                cross_sem.at[group, 3 + number],
                (three_sem if target == 3 else two_sem).at[group],
                across_to if number == 0 else pair_to,
            )
            copies[("w", group, target)] = copy

    def to_pair(key, source, target, here):
        if key not in quarters:
            quarters[key] = pltpu.make_async_remote_copy(
                src_ref=source,
                dst_ref=target,
                send_sem=quarter_sem.at[key, 0],
                recv_sem=quarter_sem.at[key, 1],
                device_id={"dp": pair_to},
                device_id_type=MESH,
            )
            partial_copies.append((None, quarters[key]))
        pl.when(here)(quarters[key].start)

    quarters = {}
    arrived = set()

    def arrive(group, position):
        if (group, position) not in arrived:
            arrived.add((group, position))
            copies[("w", group, position)].wait_recv()

    spot = pl.ds(pl.multiple_of(core * (2 * quarter) + side * quarter, quarter), quarter)
    pair_rows = pl.ds(pl.multiple_of(core * (2 * quarter), quarter), 2 * quarter)
    levels = len(spread)
    assert levels == 2

    def over_tiles(source, raw, number, work):
        def load(tile, slot):
            here = pl.ds(pl.multiple_of(tile * CHUNK, CHUNK), CHUNK)
            return pltpu.make_async_copy(source.at[here], raw.at[slot], load_sem.at[number, slot])

        load(0, 0).start()

        def one(tile, carry):
            slot = lax.rem(tile, 2)

            @pl.when(tile + 1 < length // CHUNK)
            def _():
                load(tile + 1, 1 - slot).start()

            load(tile, slot).wait()
            work(tile, slot)
            return carry

        lax.fori_loop(0, length // CHUNK, one, 0)

    outs = {}

    def leave(key, source, target, sem):
        outs[key] = pltpu.make_async_copy(source, target, sem)
        outs[key].start()

    def left(*keys):
        for key in keys:
            outs.pop(key).wait()

    def normalise(seq):
        if seq:
            copies["x3"].wait_recv()
            left(("x", 0))

        def work(tile, slot):
            here = pl.ds(pl.multiple_of(tile * CHUNK, CHUNK), CHUNK)
            both = pl.ds(pl.multiple_of(seq * length + tile * CHUNK, CHUNK), CHUNK)
            mean, inverse = stats(raw_x[slot].astype(F))
            for position, mask in enumerate(order):
                to = slice(position * part, (position + 1) * part)
                there = pl.ds(pl.multiple_of(flip(me, mask) * part, part), part)
                piece = raw_x[slot, :, there]
                normed = (piece.astype(F) - mean) * inverse
                attn_v[here, to] = (normed * vec_ref[0:1, there] + vec_ref[1:2, there]).astype(B)
                mlp_v[both, to] = (normed * vec_ref[2:3, there] + vec_ref[3:4, there]).astype(B)
                xr_v[here, to] = piece

        over_tiles(x_other if seq else x_ref, raw_x, 0, work)
        both = pl.ds(seq * length, length)
        leave(("x", seq), xr_v, x_rel.at[both], rel_sem.at[seq, 0])
        leave(("m", seq), mlp_v.at[both], mlp_out.at[both], rel_sem.at[seq, 2])

    def arrange_grad(seq):
        if seq:
            copies["g3"].wait_recv()
            left(("g", 0))
        else:
            bias_ref[...] = jnp.zeros_like(bias_ref)

        def work(tile, slot):
            here = pl.ds(pl.multiple_of(tile * CHUNK, CHUNK), CHUNK)
            if seq == 0:
                bias_ref[...] += jnp.sum(raw_g[slot].astype(F), axis=0, keepdims=True)
            for position, mask in enumerate(order):
                to = slice(position * part, (position + 1) * part)
                there = pl.ds(pl.multiple_of(flip(me, mask) * part, part), part)
                g_v[here, to] = raw_g[slot, :, there]

        over_tiles(g_other if seq else g_ref, raw_g, 1, work)
        leave(("g", seq), g_v, g_rel.at[pl.ds(seq * length, length)], rel_sem.at[seq, 1])

    def whole_group(group):
        if ("out", group) not in arrived:
            arrived.add(("out", group))
            for position in range(4, 8):
                arrive(group, position)
            leave(("w", group), w.at[group], w_out.at[group], out_sem.at[group])

    def project(seq):
        whole_group(0)

        def one(tile, carry):
            here = pl.ds(pl.multiple_of(tile * CHUNK, CHUNK), CHUNK)
            mixed = dot(attn_v[here], w[0, :, : 3 * size], ((1,), (0,)), F) + offset_ref[...]
            tables = (cos_ref[here], above_ref[here], below_ref[here])
            q_v[here] = turn(mixed[:, :size], *tables).astype(B)
            k_v[here] = turn(mixed[:, size : 2 * size], *tables).astype(B)
            v_v[here] = mixed[:, 2 * size :].astype(B)
            return carry

        lax.fori_loop(0, length // CHUNK, one, 0)

    def project_grad(seq):
        whole_group(0)
        cg_v[...] = dot(g_v[...], w[0, :, 3 * size :], ((1,), (0,)), B)

    def attend(seq):
        if seq:
            seg_copy.wait()
            left(("mg", 0), ("ctx", 0))
        scale = size ** (-0.5)
        ids = seg_ref[...] if seq == 0 else seg_v[...]
        col_v[...] = jnp.broadcast_to(ids.astype(F), (8, length)).T
        dk_v[...] = jnp.zeros_like(dk_v)
        dv_v[...] = jnp.zeros_like(dv_v)
        for first in range(0, length, QBLOCK):
            low, high = key_range(first)
            here, keys = slice(first, first + QBLOCK), slice(low, high)
            scores = dot(q_v[here], k_v[keys], ((1,), (1,)), F) * scale
            row_ids = first + lax.broadcasted_iota(jnp.int32, (QBLOCK, high - low), 0)
            key_ids = low + lax.broadcasted_iota(jnp.int32, (QBLOCK, high - low), 1)
            row = seg_ref[:, keys] if seq == 0 else seg_v[:, keys]
            allowed = (key_ids <= row_ids) & (col_v[here, 0:1] == row.astype(F))
            scores = jnp.where(allowed, scores, -1e30)
            expo = jnp.exp(scores - jnp.max(scores, axis=1, keepdims=True))
            probs = expo / jnp.sum(expo, axis=1, keepdims=True)
            low_probs = probs.astype(B)
            ctx_v[here] = dot(low_probs, v_v[keys], ((1,), (0,)), B)
            dv_v[keys] += dot(low_probs, cg_v[here], ((0,), (0,)), F)
            prob_grad = dot(cg_v[here], v_v[keys], ((1,), (1,)), F)
            centred = jnp.sum(probs * prob_grad, axis=1, keepdims=True)
            score_grad = (probs * (prob_grad - centred)).astype(B)
            q_grad = dot(score_grad, k_v[keys], ((1,), (0,)), F) * scale
            tables = (cos_ref[here], -above_ref[here], -below_ref[here])
            mg_v[here, :size] = turn(q_grad, *tables).astype(B)
            dk_v[keys] += dot(score_grad, q_v[here], ((0,), (0,)), F) * scale
        for first in range(0, length, QBLOCK):
            here = slice(first, first + QBLOCK)
            tables = (cos_ref[here], -above_ref[here], -below_ref[here])
            mg_v[here, size : 2 * size] = turn(dk_v[here], *tables).astype(B)
            mg_v[here, 2 * size :] = dv_v[here].astype(B)
        sums = jnp.sum(mg_v[...].astype(F), axis=0, keepdims=True)
        if seq == 0:
            sum_ref[...] = sums
        else:
            sum_ref[...] += sums
        both = pl.ds(seq * length, length)
        leave(("mg", seq), mg_v, mixed_out.at[both], rel_sem.at[seq, 3])
        leave(("ctx", seq), ctx_v, ctx_out.at[both], rel_sem.at[seq, 4])

    def attn_grads(seq, low, high):
        def one(block, carry):
            here = pl.ds(pl.multiple_of(block * CHUNK, CHUNK), CHUNK)
            qkv = dot(attn_v[:, here], mg_v[...], ((0,), (0,)), F)
            dense = dot(g_v[:, here], ctx_v[...], ((0,), (0,)), F)
            if seq == 0:
                grad_v[here, : 3 * size] = qkv
                grad_v[here, 3 * size :] = dense
            else:
                grad_v[here, : 3 * size] += qkv
                grad_v[here, 3 * size :] += dense
            return carry

        lax.fori_loop(low // CHUNK, high // CHUNK, one, 0)

    def up(low, high):
        def store(tile, slot):
            here = pl.ds(pl.multiple_of(tile * CHUNK, CHUNK), CHUNK)
            return (
                pltpu.make_async_copy(act_v.at[slot], act_out.at[here], tile_sem.at[0, slot]),
                pltpu.make_async_copy(slope_v.at[slot], slope_out.at[here], tile_sem.at[1, slot]),
            )

        def one(tile, carry):
            slot = lax.rem(tile, 2)
            here = pl.ds(pl.multiple_of(tile * CHUNK, CHUNK), CHUNK)
            pre = dot(mlp_v[here], w[1], ((1,), (0,)), F) + up_bias_ref[...]

            @pl.when(tile >= low + 2)
            def _():
                for copy in store(tile - 2, slot):
                    copy.wait()

            cumulative = 0.5 * (1.0 + lax.erf(pre * 0.7071067811865476))
            density = jnp.exp(-0.5 * pre * pre) * 0.3989422804014327
            act_v[slot] = (pre * cumulative).astype(B)
            slope_v[slot] = cumulative + pre * density
            for copy in store(tile, slot):
                copy.start()
            return carry

        lax.fori_loop(low, high, one, 0)
        for tile in (high - 2, high - 1):
            for copy in store(tile, tile % 2):
                copy.wait()

    seg_copy = pltpu.make_async_remote_copy(
        src_ref=seg_ref,
        dst_ref=seg_v,
        send_sem=seg_sem.at[0],
        recv_sem=seg_sem.at[1],
        device_id={"dp": pair_to},
        device_id_type=MESH,
    )
    seg_copy.start()
    kinds = {"o": outer, "i": inner}

    def relay_on(group):
        arrive(group, 1)
        relay(group)

    def send_y(group, position):
        if position:
            arrive(group, position)
        onward(group, position, 1)

    def to_side(name, number, array):
        quarters[number].wait_recv()
        remote(name + "2", array.at[spot], array.at[spot], "tensor", side_to)

    def to_core(name, array):
        copies[name + "2"].wait_recv()
        remote(name + "3", array.at[pair_rows], array.at[pair_rows], "tensor", core_to)

    def gradients(seq, number):
        middle = width // 2
        attn_grads(seq, *((0, middle) if number else (middle, width)))
        if seq and number:
            leave("keep", grad_v.at[pl.ds(0, middle)], keep_out, out_sem.at[4])
        elif seq:
            send_v[...] = grad_v[middle:].astype(B)
            leave("send", send_v, send_out, out_sem.at[3])

    def lift(seq):
        whole_group(1)
        up(seq * length // CHUNK, (seq + 1) * length // CHUNK)

    stages = {
        "sh": shard,
        "pu": lambda group, kind: pair_up(group, kinds[kind]),
        "st": straight,
        "hd": lambda group, kind: hand(group, kinds[kind]),
        "re": relay_on,
        "yo": send_y,
        "po": pass_on,
        "x1": lambda kind: to_pair(0, x_ref.at[spot], x_other.at[spot], kinds[kind]),
        "g1": lambda kind: to_pair(1, g_ref.at[spot], g_other.at[spot], kinds[kind]),
        "x2": lambda: to_side("x", 0, x_other),
        "g2": lambda: to_side("g", 1, g_other),
        "x3": lambda: to_core("x", x_other),
        "g3": lambda: to_core("g", g_other),
        "N": normalise,
        "G": arrange_grad,
        "PJ": project,
        "CG": project_grad,
        "AT": attend,
        "GR": gradients,
        "UP": lift,
    }
    for name, *numbers in GATHERING:
        stages[name](*numbers)
    whole_group(2)
    left(*list(outs))
    for key, copy in copies.items():
        if key[0] != "w" or key[2] not in (2, 3):
            copy.wait_send()
    for here, copy in partial_copies:
        if here is None:
            copy.wait_send()
        else:
            pl.when(here)(copy.wait_send)


SCHEDULE = (
    ("pre", 1),
    ("st", 1, 1),
    ("yf", 0, 3),
    ("kt", 1, 1),
    ("ps", 2),
    ("yf", 0, 2),
    ("st", 0, 1),
    ("yn", 0, 1),
    ("kt", 0, 1),
    ("po", 0, 1),
    ("es", 1),
    ("st", 1, 0),
    ("po", 0, 2),
    ("po", 0, 0),
    ("pk", 2),
    ("kt", 1, 0),
    ("pre", 0),
    ("yf", 2, 3),
    ("st", 0, 0),
    ("yn", 0, 0),
    ("yf", 2, 2),
    ("kt", 0, 0),
    ("sb",),
    ("es", 0),
    ("po", 2, 1),
    ("ps", 1),
    ("se", 0),
    ("zl", 0, 1),
    ("zl", 0, 0),
    ("po", 2, 0),
    ("pk", 1),
    ("yf", 1, 3),
    ("fin", 1),
    ("yn", 2, 0),
    ("se", 1),
    ("yf", 1, 2),
    ("yn", 2, 1),
    ("po", 2, 2),
    ("zl", 2, 1),
    ("fin", 0),
    ("fa", 0),
    ("po", 1, 1),
    ("yn", 1, 0),
    ("po", 1, 2),
    ("yn", 1, 1),
    ("po", 1, 0),
    ("se", 2),
    ("zl", 1, 1),
    ("zl", 1, 0),
    ("fa", 2),
    ("fe", 1),
    ("fe", 0),
    ("zl", 2, 0),
    ("se", 3),
    ("se", 4),
    ("fa", 1),
)

def scatter_kernel(
    groups,
    attn_send,
    attn_keep,
    weights,
    x_rel,
    g_rel,
    mlp_in,
    mixed_grad,
    context,
    activation,
    slope,
    x_ref,
    g_ref,
    vec_ref,
    mixed_sum,
    bias_sum,
    block_out,
    input_grad,
    qkv_out,
    dense_out,
    up_out,
    down_out,
    far_in,
    far_two,
    y_recv,
    z_recv,
    z_relay,
    c_recv,
    x_recv,
    e_recv,
    small_out,
    w,
    act_v,
    pre_v,
    tile_v,
    col_v,
    slope_t,
    mix_t,
    ctx_v,
    keep_v,
    y_send,
    z_send,
    p_send,
    y_stage,
    c_send,
    c_stage,
    r_stage,
    x_send,
    hold_v,
    mean_v,
    inverse_v,
    sum_v,
    small_v,
    small_recv,
    load_sem,
    tile_sem,
    ys_sem,
    yr_sem,
    zs_sem,
    zr_sem,
    zl_sem,
    zf_sem,
    two_sem,
    ps_sem,
    pr_sem,
    cs_sem,
    cr_sem,
    xs_sem,
    xr_sem,
    es_sem,
    er_sem,
    fs_sem,
    fr_sem,
    emit_sem,
    ss_sem,
    sr_sem,
    out_sem,
):
    length, width = x_ref.shape
    part = width // groups
    size = context.shape[1]
    hidden = activation.shape[1]
    quarter = length // 4
    me, place = lax.axis_index("dp"), lax.axis_index("tensor")
    core, side, half = lax.rem(place, 2), lax.div(place, 2), bit_of(me, PAIR)
    pair_to, side_to, core_to = flip(me, PAIR), flip(place, 2), flip(place, 1)
    spread, order = block_order(groups)
    z_to, y_to = [flip(me, bit) for bit in spread]
    across_to = flip(z_to, PAIR)
    inner = bit_of(me, PAIR) != bit_of(me, spread[0])
    outer = bit_of(me, PAIR) == bit_of(me, spread[0])
    greet([("dp", to) for to in (pair_to, z_to, y_to, across_to)] + [("tensor", side_to), ("tensor", core_to)])

    def remote(source, target, send, recv, axis, index):
        return pltpu.make_async_remote_copy(
            src_ref=source, dst_ref=target, send_sem=send, recv_sem=recv, device_id={axis: index}, device_id_type=MESH
        )

    def span(position, count=1):
        return pl.ds(position * part, count * part)

    def step(index, amount):
        return pl.ds(pl.multiple_of(index * amount, amount), amount)

    def y_copy(group, position):
        source = attn_send if group == 0 else y_send
        here = step(position, part) if not isinstance(position, int) else span(position)
        return remote(
            source.at[here], y_recv.at[group, here], ys_sem.at[group, position], yr_sem.at[group, position], "dp", y_to
        )

    slot_of = (0, 0, 1)

    def z_copy(group, position):
        source, sem = z_send.at[slot_of[group], span(position - 2)], zs_sem.at[group, position - 2]
        onward = (
            remote(source, far_two.at[group], sem, two_sem.at[group], "dp", across_to)
            if position == 3
            else remote(source, z_relay.at[group, span(2)], sem, zl_sem.at[group, 2], "dp", across_to)
        )
        aside = remote(
            source, z_relay.at[group, span(position - 2)], sem, zl_sem.at[group, position - 2], "dp", pair_to
        )
        return onward, aside

    def forward(group, number):
        target = 0 if number == 2 else number
        arrived = remote(
            z_relay.at[group, span(number)],
            z_recv.at[group, span(target)],
            zf_sem.at[group, number],
            zl_sem.at[group, number],
            "dp",
            pair_to,
        )
        return arrived, remote(
            z_relay.at[group, span(number)],
            z_recv.at[group, span(target)],
            zf_sem.at[group, number],
            zr_sem.at[group, target],
            "dp",
            pair_to if number == 2 else across_to,
        )

    def pass_on(group, *numbers):
        @pl.when(inner)
        def _():
            for number in numbers:
                arrived, copy = forward(group, number)
                arrived.wait_recv()
                copy.start()

    def z_arrived(group, position):
        return remote(
            z_relay.at[group, span(position)],
            z_recv.at[group, span(position)],
            zf_sem.at[group, position],
            zr_sem.at[group, position],
            "dp",
            pair_to,
        )

    def p_copy(group):
        return remote(
            p_send.at[slot_of[group]], far_in.at[group], ps_sem.at[group], pr_sem.at[group], "dp", pair_to
        )

    emitted = {}

    def emit(group, kind, block, owner):
        copies = []
        for number in range(hidden // part):
            at = pl.ds(number * part, part)
            if group == 2 or (group == 0 and number == 3):
                block[:, at] = block[:, at].T
            if group == 1:
                target = up_out.at[:, pl.ds(pl.multiple_of(owner * hidden + number * part, part), part)]
            elif group == 2:
                target = down_out.at[pl.ds(pl.multiple_of(owner * hidden + number * part, part), part)]
            elif number == 3:
                target = dense_out.at[owner]
            else:
                target = qkv_out.at[:, pl.ds(pl.multiple_of(owner * 3 * size + number * part, part), part)]
            copies.append(pltpu.make_async_copy(block.at[:, at], target, emit_sem.at[group, kind, number]))
            copies[-1].start()
        emitted[(group, kind)] = copies

    def emit_near(group):
        emit(group, 0, keep_v.at[slot_of[group], span(0)], half)

    def emit_far(group):
        block = (
            hold_v.at[1, 1, :, pl.ds(0, hidden)],
            keep_v.at[0, span(1)],
            hold_v.at[1, 1, :, pl.ds(hidden, hidden)],
        )[group]
        p_copy(group).wait_recv()
        staged(far_in.at[group])
        block[...] = y_stage[...].astype(F)

        @pl.when(inner)
        def _():
            remote(
                p_send.at[0], far_two.at[group], two_sem.at[group], two_sem.at[group], "dp", across_to
            ).wait_recv()
            staged(far_two.at[group])
            block[...] += y_stage[...].astype(F)

        emit(group, 1, block, 1 - half)

    def staged(source):
        copy = pltpu.make_async_copy(source, y_stage, load_sem.at[6])
        copy.start()
        copy.wait()

    def y_far(group, position):
        if group == 0:
            need(5)
        y_copy(group, position).wait_recv()
        staged(y_recv.at[group, span(position)])
        total = keep_v[slot_of[group], span(position)] + y_stage[...].astype(F)
        onward, aside = z_copy(group, position)
        if group == 1:
            z_copy(0, position)[0].wait_send()
        z_send[slot_of[group], span(position - 2)] = total.astype(B)
        pl.when(inner)(onward.start)
        pl.when(outer)(aside.start)

    def y_near(group, position):
        if group == 0:
            need(5)
        y_copy(group, position).wait_recv()
        staged(y_recv.at[group, span(position)])
        total = keep_v[slot_of[group], span(position)] + y_stage[...].astype(F)
        keep_v[slot_of[group], span(position)] = total
        if position == 1:
            if group == 1:
                p_copy(0).wait_send()

            @pl.when(outer)
            def _():
                p_send[slot_of[group]] = keep_v[slot_of[group], span(1)].astype(B)
                p_copy(group).start()

    def z_last(group, position):
        def add():
            z_arrived(group, position).wait_recv()
            staged(z_recv.at[group, span(position)])
            return keep_v[slot_of[group], span(position)] + y_stage[...].astype(F)

        if position == 1:

            @pl.when(inner)
            def _():
                p_send[slot_of[group]] = add().astype(B)
                p_copy(group).start()

        else:
            keep_v[slot_of[group], span(0)] = add()
            emit_near(group)

    loads = [
        pltpu.make_async_copy(weights.at[2], w.at[2], load_sem.at[0]),
        pltpu.make_async_copy(weights.at[0], w.at[0], load_sem.at[1]),
        pltpu.make_async_copy(weights.at[1], w.at[1], load_sem.at[2]),
        pltpu.make_async_copy(activation, act_v, load_sem.at[3]),
        pltpu.make_async_copy(context, ctx_v, load_sem.at[4]),
        pltpu.make_async_copy(attn_keep, keep_v.at[0], load_sem.at[5]),
    ]
    for number in (4, 3, 1, 0, 5, 2):
        loads[number].start()
    loaded = set()

    def need(*numbers):
        for number in numbers:
            if number not in loaded:
                loaded.add(number)
                loads[number].wait()

    for position in (3, 2, 1, 0):
        y_copy(0, position).start()

    small_v[...] = jnp.zeros_like(small_v)

    def pre_load(tile, slot):
        here = step(tile, CHUNK)
        return (
            pltpu.make_async_copy(g_rel.at[here], tile_v.at[step(slot, CHUNK)], tile_sem.at[0, slot]),
            pltpu.make_async_copy(slope.at[here], slope_t.at[slot], tile_sem.at[1, slot]),
        )

    sum_v[...] = jnp.zeros_like(sum_v)

    def pre_tiles(seq):
        need(0)
        low, high = seq * length // CHUNK, (seq + 1) * length // CHUNK
        for copy in pre_load(low, 0):
            copy.start()

        def one(tile, carry):
            slot = lax.rem(tile, 2)

            @pl.when(tile + 1 < high)
            def _():
                for copy in pre_load(tile + 1, 1 - slot):
                    copy.start()

            for copy in pre_load(tile, slot):
                copy.wait()
            grad = (dot(tile_v[step(slot, CHUNK)], w[2], ((1,), (0,)), F) * slope_t[slot]).astype(B)
            pre_v[step(tile, CHUNK)] = grad
            sum_v[...] += jnp.sum(grad.astype(F), axis=0, keepdims=True)
            return carry

        lax.fori_loop(low, high, one, 0)

    tall = 2 * quarter
    blocks = width // CHUNK

    def c_copy(which, seq, block):
        here = step(block, CHUNK)
        return remote(
            c_send.at[:, here],
            c_recv.at[which, seq, :, here],
            cs_sem.at[which, seq, block],
            cr_sem.at[which, seq, block],
            "tensor",
            core_to,
        )

    def x_copy(which, seq):
        return remote(
            x_send.at[which, seq], x_recv.at[which, seq], xs_sem.at[which, seq], xr_sem.at[which, seq], "tensor", side_to
        )

    def e_copy(which):
        return remote(x_send.at[which, 1], e_recv.at[which], es_sem.at[which], er_sem.at[which], "dp", pair_to)

    sent_tiles = []

    def send_tile(which, seq):
        begin, block_of = tile_of[which]
        need(*((1, 2) if which == 0 else (0, 1, 3, 4)))
        start = pl.multiple_of(seq * length + (1 - core) * tall, tall)
        begin(start)

        def one(block, carry):
            value = block_of(start, block)
            if sent_tiles:
                c_copy(*sent_tiles[-1], block).wait_send()
            c_send[:, step(block, CHUNK)] = value.astype(B)
            c_copy(which, seq, block).start()
            return carry

        lax.fori_loop(0, blocks, one, 0)
        sent_tiles.append((which, seq))

    def c_load(which, seq, block, slot):
        return pltpu.make_async_copy(c_recv.at[which, seq, :, step(block, CHUNK)], c_stage.at[slot], tile_sem.at[2, slot])

    def keep_tile(which, seq):
        begin, block_of = tile_of[which]
        start = pl.multiple_of(seq * length + core * tall, tall)
        begin(start)
        c_copy(which, seq, 0).wait_recv()
        c_load(which, seq, 0, 0).start()

        def one(block, carry):
            slot = lax.rem(block, 2)
            value = block_of(start, block)

            @pl.when(block + 1 < blocks)
            def _():
                c_copy(which, seq, block + 1).wait_recv()
                c_load(which, seq, block + 1, 1 - slot).start()

            c_load(which, seq, block, slot).wait()
            r_stage[...] = value + c_stage[slot].astype(F)
            here = step(block, CHUNK)
            hold_v[which, seq, :, here] = r_stage[step(side, quarter)]
            x_send[which, seq, :, here] = r_stage[step(1 - side, quarter)].astype(B)
            return carry

        lax.fori_loop(0, blocks, one, 0)
        x_copy(which, seq).start()

    def blend_begin(start):
        copies = (
            pltpu.make_async_copy(x_rel.at[pl.ds(start, tall)], tile_v, tile_sem.at[3, 0]),
            pltpu.make_async_copy(mixed_grad.at[pl.ds(start, tall)], mix_t, tile_sem.at[3, 1]),
        )
        for copy in copies:
            copy.start()
        for copy in copies:
            copy.wait()
        for slot in range(2):
            mean, inverse = stats(tile_v[span_rows(slot)].astype(F))
            mean_v[span_rows(slot)] = jnp.broadcast_to(mean, (CHUNK, 128))
            inverse_v[span_rows(slot)] = jnp.broadcast_to(inverse, (CHUNK, 128))

    def span_rows(slot):
        return pl.ds(slot * CHUNK, CHUNK)

    def natural_block(position):
        result = me
        for level, bit in enumerate([PAIR] + spread):
            flipped = lax.rem(lax.div(position, 1 << level), 2)
            result = result + bit * (1 - 2 * bit_of(me, bit)) * flipped
        return result

    def blend_block(start, block):
        here = step(block, CHUNK)
        there = step(natural_block(block), part)
        attn_grad = dot(mix_t[...], w[0, here, : 3 * size], ((1,), (1,)), F)
        mlp_grad = dot(pre_v[pl.ds(start, tall)], w[1, here, :], ((1,), (1,)), F)
        mean, inverse = mean_v[...], inverse_v[...]
        mean = jnp.concatenate([mean] * (CHUNK // 128), axis=1)
        inverse = jnp.concatenate([inverse] * (CHUNK // 128), axis=1)
        normed = (tile_v[:, here].astype(F) - mean) * inverse
        small_v[0:1, there] += jnp.sum(attn_grad * normed, axis=0, keepdims=True)
        small_v[1:2, there] += jnp.sum(attn_grad, axis=0, keepdims=True)
        small_v[2:3, there] += jnp.sum(mlp_grad * normed, axis=0, keepdims=True)
        small_v[3:4, there] += jnp.sum(mlp_grad, axis=0, keepdims=True)
        return attn_grad * vec_ref[0:1, there] + mlp_grad * vec_ref[2:3, there]

    def product(columns, right, group, positions, sent, old=None):
        count = len(positions)
        base = positions[0]
        sign = positions[1] - positions[0] if count > 1 else 1

        def load(number, slot):
            return pltpu.make_async_copy(
                columns.at[:, step(base + sign * number, part)], col_v.at[slot], tile_sem.at[4, slot]
            )

        load(0, 0).start()

        def one(number, carry):
            slot = lax.rem(number, 2)

            @pl.when(number + 1 < count)
            def _():
                load(number + 1, 1 - slot).start()

            load(number, slot).wait()
            value = dot(col_v[slot], right[...], ((0,), (0,)), F)
            position = base + sign * number
            if sent:
                if old is not None:
                    y_copy(old, position - groups // 2).wait_send()
                y_send[step(position - groups // 2, part)] = value.astype(B)
                y_copy(group, position - groups // 2).start()
            else:
                keep_v[slot_of[group], step(position, part)] = value
            return carry

        lax.fori_loop(0, count, one, 0)

    def small_begin():
        small_v[4:5] = bias_sum[...]
        small_v[5:6, step(half, hidden)] = sum_v[...]
        small_v[6:7, pl.ds(pl.multiple_of(half * (width // 2), width // 2), 3 * size)] = mixed_sum[...]
        small_copy(0).start()

    rounds = [("dp", flip(me, bit)) for bit in [PAIR] + spread] + [("tensor", side_to), ("tensor", core_to)]

    def small_copy(number):
        return remote(small_v, small_recv.at[number], ss_sem.at[number], sr_sem.at[number], *rounds[number])

    def small_end(number):
        small_copy(number).wait()
        if number < 3:
            small_v[...] += small_recv[number]
        else:
            small_v[0:4] += small_recv[number, 0:4]
        if number + 1 < len(rounds):
            small_copy(number + 1).start()

    def branch_begin(start):
        pass

    def branch_block(start, block):
        here, rows = step(block, CHUNK), pl.ds(start, tall)
        return dot(ctx_v[rows], w[0, here, 3 * size :], ((1,), (1,)), F) + dot(
            act_v[rows], w[2, here, :], ((1,), (1,)), F
        )

    def read_stage(source):
        copy = pltpu.make_async_copy(source, tile_v.at[pl.ds(0, quarter)], load_sem.at[6])
        copy.start()
        copy.wait()

    def e_start(which):
        x_copy(which, 1).wait_recv()
        x_copy(which, 1).wait_send()
        read_stage(x_recv.at[which, 1])

        def one(block, carry):
            here = step(block, CHUNK)
            x_send[which, 1, :, here] = (hold_v[which, 1, :, here] + tile_v[0:quarter, here].astype(F)).astype(B)
            return carry

        lax.fori_loop(0, blocks, one, 0)
        e_copy(which).start()

    def gather_own(which):
        x_copy(which, 0).wait_recv()
        read_stage(x_recv.at[which, 0])

        def one(block, carry):
            here = step(block, CHUNK)
            hold_v[which, 0, :, here] += tile_v[0:quarter, here].astype(F)
            return carry

        lax.fori_loop(0, blocks, one, 0)

    def spot(c, s):
        return pl.ds(pl.multiple_of(c * tall + s * quarter, quarter), quarter)

    def position_of(block, shifted=False):
        result = 0
        for level, bit in enumerate([PAIR] + spread):
            mine = bit_of(me, bit)
            if shifted and bit == PAIR:
                mine = 1 - mine
            result = result + (1 << level) * ((1 - mine) if block & bit else mine)
        return result

    def finish(which, out_ref):
        if len(sent_tiles) == 4:
            sent_tiles.append(None)
            for block in range(blocks):
                c_copy(*sent_tiles[3], block).wait_send()
        gather_own(which)
        e_copy(which).wait_recv()
        copies = [
            pltpu.make_async_copy(e_recv.at[which], tile_v.at[pl.ds(0, quarter)], load_sem.at[6]),
            pltpu.make_async_copy(x_ref.at[spot(core, side)], tile_v.at[pl.ds(quarter, quarter)], load_sem.at[7]),
        ]
        if which == 0:
            copies.append(pltpu.make_async_copy(g_ref.at[spot(core, side)], x_send.at[0, 0], load_sem.at[8]))
            x_copy(0, 0).wait_send()
        for copy in copies:
            copy.start()
        for copy in copies:
            copy.wait()
        here = pl.ds(which * quarter, quarter)
        if which == 0:
            total_u, total_un = 0.0, 0.0
            mean, inverse = stats(tile_v[quarter:].astype(F))
            for block in range(groups):
                mine = hold_v[0, 0, :, step(position_of(block), part)]
                theirs = tile_v[0:quarter, step(position_of(block, True), part)].astype(F)
                blend = mine + theirs
                normed = (tile_v[quarter:, block * part : (block + 1) * part].astype(F) - mean) * inverse
                hold_v[0, 1, :, block * part : (block + 1) * part] = blend
                total_u = total_u + jnp.sum(blend, axis=1, keepdims=True)
                total_un = total_un + jnp.sum(blend * normed, axis=1, keepdims=True)
            mean_u, mean_un = total_u * (1.0 / width), total_un * (1.0 / width)
            for block in range(groups):
                at = slice(block * part, (block + 1) * part)
                normed = (tile_v[quarter:, at].astype(F) - mean) * inverse
                inner = (hold_v[0, 1, :, at] - mean_u - normed * mean_un) * inverse
                c_send[here, at] = (x_send[0, 0, :, at].astype(F) + inner).astype(B)
        else:
            for block in range(groups):
                at = slice(block * part, (block + 1) * part)
                mine = hold_v[1, 0, :, step(position_of(block), part)]
                theirs = tile_v[0:quarter, step(position_of(block, True), part)].astype(F)
                bias = vec_ref[4:5, at] + vec_ref[5:6, at]
                c_send[here, at] = (tile_v[quarter:, at].astype(F) + (mine + theirs) + bias).astype(B)
        first = remote(
            c_send.at[here], out_ref.at[spot(core, side)], fs_sem.at[which, 0], fr_sem.at[which, 0], "tensor", side_to
        )
        second = remote(
            c_send.at[here], out_ref.at[spot(core, side)], fs_sem.at[which, 1], fr_sem.at[which, 1], "tensor", core_to
        )
        own = pltpu.make_async_copy(c_send.at[here], out_ref.at[spot(core, side)], out_sem.at[3 + which])
        for copy in (first, second, own):
            copy.start()
        return first, second, own

    def finish_end(which, out_ref, copies):
        first, second, own = copies
        first.wait_recv()
        third = remote(
            out_ref.at[spot(core, 1 - side)],
            out_ref.at[spot(core, 1 - side)],
            fs_sem.at[which, 2],
            fr_sem.at[which, 2],
            "tensor",
            core_to,
        )
        third.start()
        return [first.wait_send, second.wait, third.wait, own.wait]

    tile_of = ((blend_begin, blend_block), (branch_begin, branch_block))
    outs, finished, ends = (input_grad, block_out), {}, []

    def do_product(group, sent):
        columns, right = ((mlp_in, pre_v), (g_rel, act_v))[group - 1]
        if group == 2:
            need(3)
        if group == 1 and not sent:
            for copy in emitted[(0, 0)]:
                copy.wait()
        product(columns, right, group, (7, 6, 5, 4) if sent else (3, 2, 1, 0), sent, 2 if sent and group == 1 else None)

    def do_finish(which):
        finished[which] = finish(which, outs[which])

    def do_end(which):
        ends.extend(finish_end(which, outs[which], finished[which]))

    stages = {
        "pre": pre_tiles,
        "st": send_tile,
        "kt": keep_tile,
        "ps": lambda group: do_product(group, True),
        "pk": lambda group: do_product(group, False),
        "yf": y_far,
        "yn": y_near,
        "po": pass_on,
        "zl": z_last,
        "es": e_start,
        "fin": do_finish,
        "fe": do_end,
        "fa": emit_far,
        "sb": small_begin,
        "se": small_end,
    }
    for name, *numbers in SCHEDULE:
        stages[name](*numbers)
    small_out[...] = small_v[...]
    for end in ends:
        end()
    for group in range(3):
        if group:
            p_copy(group).wait_send()
            for position in (2, 3):
                z_copy(group, position)[0].wait_send()
        for position in range(4):
            if group != 2:
                y_copy(group, position).wait_send()
        for kind in range(2):
            if group or kind:
                for copy in emitted[(group, kind)]:
                    copy.wait()

        @pl.when(inner)
        def _():
            for number in range(3):
                forward(group, number)[1].wait_send()

    for which in range(2):
        e_copy(which).wait_send()
        if which:
            x_copy(which, 0).wait_send()


def body_narrow(
    tokens,
    segment_ids,
    out_grad,
    attn_norm_gain,
    attn_norm_bias,
    mlp_norm_gain,
    mlp_norm_bias,
    qkv_weight,
    qv_bias,
    key_bias,
    dense_weight,
    dense_bias,
    up_weight,
    up_bias,
    down_weight,
    down_bias,
    *,
    groups,
    ways,
):
    length, width = tokens.shape[1:]
    heads, size = qkv_weight.shape[1] // 2, qkv_weight.shape[3]
    part = width // groups
    me = lax.axis_index("dp")
    half = (me // PAIR) % 2
    place = lax.axis_index("tensor")
    core, side = place % 2, place // 2
    spread = [bit for bit in (1 << k for k in reversed(range(groups.bit_length() - 1))) if bit != PAIR]

    def swap(array, bit):
        return lax.ppermute(array, "dp", [(i, i ^ bit) for i in range(groups)])

    def cross(array, bit):
        return lax.ppermute(array, "tensor", [(i, i ^ bit) for i in range(ways)])

    def pick(array, index, axis, count=2):
        rows = array.shape[axis] // count
        return lax.dynamic_slice_in_dim(array, index * rows, rows, axis)

    def join(mine, theirs, index, axis):
        pair = jnp.concatenate([mine, theirs], axis=axis)
        turned = jnp.concatenate([theirs, mine], axis=axis)
        return jnp.where(index == 0, pair, turned)

    order = [0, PAIR]
    for bit in spread:
        order = order + [mask | bit for mask in order]
    inverse = [order.index(mask) for mask in range(groups)]

    def arranged(array):
        return jnp.concatenate(
            [lax.dynamic_slice_in_dim(array, (mask ^ me) * part, part, array.ndim - 1) for mask in order], axis=-1
        )

    def natural(array):
        table = jnp.asarray(inverse, jnp.int32)
        return jnp.concatenate(
            [lax.dynamic_slice_in_dim(array, table[block ^ me] * part, part, array.ndim - 1) for block in range(groups)],
            axis=-1,
        )

    def gather(shard, halves_axis, axis):
        shard = shard.astype(B)
        mine, theirs = pick(shard, half, halves_axis), pick(shard, 1 - half, halves_axis)
        pieces = [jnp.concatenate([mine, swap(theirs, PAIR)], axis=axis)]
        for bit in spread:
            pieces = pieces + [swap(piece, bit) for piece in pieces]
        return jnp.concatenate(pieces, axis=axis)

    def scatter(product, axis, halves_axis):
        count = groups // 2
        sent = swap(product(count, groups, B), spread[-1])
        held = product(0, count, F) + sent.astype(F)
        for bit in reversed(spread[:-1]):
            keep, send = jnp.split(held, 2, axis=axis)
            held = keep + swap(send.astype(B), bit).astype(F)
        keep, send = jnp.split(held, 2, axis=axis)
        return join(keep, swap(send, PAIR), half, halves_axis)

    def share_rows(rows):
        rows = join(rows, cross(rows, 2), side, 0)
        return join(rows, cross(rows, 1), core, 0)

    def own_rows(array, axis):
        return pick(pick(array, core, axis), side, axis)

    def partner_rows(array):
        return share_rows(swap(own_rows(array, 0), PAIR))

    def total_rows(partial):
        held = pick(partial, core, 1).astype(F) + cross(pick(partial, 1 - core, 1), 1).astype(F)
        held = pick(held, side, 1) + cross(pick(held, 1 - side, 1).astype(B), 2).astype(F)
        sent = swap(held[1].astype(B), PAIR).astype(F)
        rows = sent.shape[0]
        sent = jnp.flip(sent.reshape(rows, groups // 2, 2, part), axis=2).reshape(rows, width)
        return held[0] + sent

    own_x, own_g = tokens[0], out_grad[0]
    w_up = gather(up_weight, 1, 0)
    x_other = partner_rows(own_x)
    w_down = gather(down_weight, 0, 1)
    g_other = partner_rows(own_g)
    w_qkv = gather(qkv_weight.reshape(part, 2, -1), 1, 0).reshape(width, -1)
    w_dense = gather(dense_weight.reshape(2 * heads * size, part), 0, 1)

    x_pair = arranged(jnp.concatenate([own_x, x_other], axis=0))
    g_pair = arranged(jnp.concatenate([own_g, g_other], axis=0))
    gains = [arranged(v) for v in (attn_norm_gain, attn_norm_bias, mlp_norm_gain, mlp_norm_bias)]

    def hat(rows):
        rows = rows.astype(F)
        center = rows - jnp.mean(rows, axis=-1, keepdims=True)
        inverse_dev = lax.rsqrt(jnp.mean(center * center, axis=-1, keepdims=True) + 1e-05)
        return center * inverse_dev, inverse_dev

    normed, _ = hat(x_pair)
    attn_in = (normed * gains[0] + gains[1]).astype(B)
    mlp_in = (normed * gains[2] + gains[3]).astype(B)

    up_here = pick(up_bias, half, 0)
    up_pre = dot(mlp_in, w_up, ((1,), (0,)), F) + up_here
    activation = jax.nn.gelu(up_pre, approximate=False).astype(B)
    middle = width // 2

    def columns(array, low, high):
        return array[:, low * part : high * part]

    down_shard = scatter(lambda low, high, kind: dot(activation, columns(g_pair, low, high), ((0,), (0,)), kind), 1, 0)
    pre_grad = (dot(g_pair, w_down, ((1,), (1,)), F) * gelu_slope(up_pre)).astype(B)
    up_shard = scatter(lambda low, high, kind: dot(columns(mlp_in, low, high), pre_grad, ((0,), (0,)), kind), 0, 1)
    up_bias_sum = jnp.sum(pre_grad.astype(F), axis=0)

    seg_other = swap(segment_ids[0], PAIR)
    seg = jnp.stack([segment_ids[0], seg_other])
    seg_col, seg_row = seg[:, :, None], seg[:, None, :]
    qv_here, key_here = pick(qv_bias, half, 0), pick(key_bias, half, 0)
    key_full = jnp.concatenate([key_here, jnp.zeros((heads, size - ROT), F)], axis=1)
    offsets = jnp.stack([qv_here[:, 0], key_full, qv_here[:, 1]], axis=1).reshape(heads, 1, 3 * size)
    mixed = dot(attn_in, w_qkv, ((1,), (0,)), F).reshape(2, length, heads, 3 * size)
    tables = rope_tables(length)
    table_specs = [shared(length, 128)] * 3
    seg_specs = [per_seq(length, 1), per_seq(1, length)]
    context_grad = dot(g_pair, w_dense, ((1,), (1,)), B).reshape(2, length, heads, size)
    contexts, mixed_grads, mixed_sums = [], [], []
    head_shape = jax.ShapeDtypeStruct((2, length, size), B)
    for head in range(heads):
        q, k, v, context, lse = pl.pallas_call(
            attn_forward,
            grid=(2,),
            in_specs=[per_seq(length, 3 * size), shared(1, 3 * size)] + table_specs + seg_specs,
            out_specs=[per_seq(length, size)] * 4 + [per_seq(length, 1)],
            out_shape=[head_shape] * 4 + [jax.ShapeDtypeStruct((2, length, 1), F)],
            name="attn_forward",
        )(mixed[:, :, head], offsets[head], *tables, seg_col, seg_row)
        mixed_grad, mixed_sum = pl.pallas_call(
            attn_backward,
            grid=(2,),
            in_specs=[per_seq(length, size)] * 4 + [per_seq(length, 1)] + table_specs + seg_specs,
            out_specs=[per_seq(length, 3 * size), per_seq(1, 3 * size)],
            out_shape=[
                jax.ShapeDtypeStruct((2, length, 3 * size), B),
                jax.ShapeDtypeStruct((2, 1, 3 * size), F),
            ],
            scratch_shapes=[pltpu.VMEM((length, size), F)] * 3,
            name="attn_backward",
        )(q, k, v, context_grad[:, :, head], lse, *tables, seg_col, seg_row)
        contexts.append(context.reshape(2 * length, size))
        mixed_grads.append(mixed_grad.reshape(2 * length, 3 * size))
        mixed_sums.append(jnp.sum(mixed_sum, axis=(0, 1)))
    context = jnp.concatenate(contexts, axis=1)
    mixed_grad = jnp.concatenate(mixed_grads, axis=1)
    mixed_sum = jnp.stack(mixed_sums).reshape(heads, 3, size)

    qkv_shard = scatter(lambda low, high, kind: dot(columns(attn_in, low, high), mixed_grad, ((0,), (0,)), kind), 0, 1)
    dense_shard = scatter(lambda low, high, kind: dot(context, columns(g_pair, low, high), ((0,), (0,)), kind), 1, 0)

    branch = dot(context, w_dense, ((1,), (0,)), F) + dot(activation, w_down, ((1,), (0,)), F)
    branch_rows = total_rows(branch.astype(B).reshape(2, length, width))
    x_rows, g_rows = own_rows(x_pair[:length], 0), own_rows(g_pair[:length], 0)
    out_rows = (x_rows.astype(F) + branch_rows + arranged(dense_bias) + arranged(down_bias)).astype(B)
    block_out = share_rows(natural(out_rows))

    attn_in_grad = dot(mixed_grad, w_qkv, ((1,), (1,)), F)
    mlp_in_grad = dot(pre_grad, w_up, ((1,), (1,)), F)
    blend = (attn_in_grad * gains[0] + mlp_in_grad * gains[2]).astype(B)
    blend_rows = total_rows(blend.reshape(2, length, width))
    hat_rows, inverse_rows = hat(x_rows)
    inner = (
        blend_rows
        - jnp.mean(blend_rows, axis=-1, keepdims=True)
        - hat_rows * jnp.mean(blend_rows * hat_rows, axis=-1, keepdims=True)
    )
    input_grad = share_rows(natural((g_rows.astype(F) + inner * inverse_rows).astype(B)))

    norm_sums = natural(
        jnp.stack(
            [
                jnp.sum(attn_in_grad * normed, axis=0),
                jnp.sum(attn_in_grad, axis=0),
                jnp.sum(mlp_in_grad * normed, axis=0),
                jnp.sum(mlp_in_grad, axis=0),
            ]
        )
    ).reshape(-1)
    bias_sum = jnp.sum(own_g.astype(F), axis=0)

    def slotted(array):
        zero = jnp.zeros_like(array)
        return join(array, zero, half, 0)

    small = [norm_sums, bias_sum, slotted(up_bias_sum), slotted(mixed_sum).reshape(-1)]
    sizes = [s.shape[0] for s in small]
    flat = jnp.concatenate(small)
    for bit in [1 << k for k in range(groups.bit_length() - 1)]:
        flat = flat + swap(flat, bit)
    ends = [sum(sizes[: i + 1]) for i in range(len(sizes))]
    norms = flat[: ends[0]]
    for bit in [1 << k for k in range(ways.bit_length() - 1)]:
        norms = norms + cross(norms, bit)
    norms = norms.reshape(4, width)
    bias_grad = flat[ends[0] : ends[1]]
    up_bias_grad = flat[ends[1] : ends[2]]
    mixed_bias = flat[ends[2] :].reshape(2 * heads, 3, size)
    qv_grad = jnp.stack([mixed_bias[:, 0], mixed_bias[:, 2]], axis=1)
    key_bias_grad = mixed_bias[:, 1, :ROT]

    return (
        block_out[None],
        input_grad[None],
        norms[0],
        norms[1],
        norms[2],
        norms[3],
        qkv_shard.reshape(qkv_weight.shape),
        qv_grad,
        key_bias_grad,
        dense_shard.reshape(dense_weight.shape),
        bias_grad,
        up_shard,
        up_bias_grad,
        down_shard,
        bias_grad,
    )


def body(
    tokens,
    segment_ids,
    out_grad,
    attn_norm_gain,
    attn_norm_bias,
    mlp_norm_gain,
    mlp_norm_bias,
    qkv_weight,
    qv_bias,
    key_bias,
    dense_weight,
    dense_bias,
    up_weight,
    up_bias,
    down_weight,
    down_bias,
    *,
    groups,
    ways,
):
    length, width = tokens.shape[1:]
    heads, size = qkv_weight.shape[1] // 2, qkv_weight.shape[3]
    assert heads == 1 and ways == 4
    part = width // groups
    hidden = up_weight.shape[1] // 2
    count = 2 * length
    me = lax.axis_index("dp")
    half = (me // PAIR) % 2
    shape = jax.ShapeDtypeStruct

    def pick(array, index, axis):
        rows = array.shape[axis] // 2
        return lax.dynamic_slice_in_dim(array, index * rows, rows, axis)

    vectors = jnp.stack([attn_norm_gain, attn_norm_bias, mlp_norm_gain, mlp_norm_bias, dense_bias, down_bias])
    own_x, own_g = tokens[0], out_grad[0]

    qv_here, key_here = pick(qv_bias, half, 0), pick(key_bias, half, 0)
    key_full = jnp.concatenate([key_here, jnp.zeros((heads, size - ROT), F)], axis=1)
    offsets = jnp.stack([qv_here[:, 0], key_full, qv_here[:, 1]], axis=1).reshape(1, 3 * size)
    tables = rope_tables(length)
    up_here = pick(up_bias, half, 0)[None]
    columns = hidden
    half_width = width // 2
    vmem, hbm = pl.BlockSpec(memory_space=pltpu.VMEM), pl.BlockSpec(memory_space=pl.ANY)
    (
        weights,
        _,
        _,
        _,
        x_pair,
        g_pair,
        mlp_in,
        mixed_grad,
        context,
        activation,
        slope,
        attn_send,
        attn_keep,
        mixed_sum,
        bias_sum,
    ) = pl.pallas_call(
        functools.partial(gather_kernel, groups),
        in_specs=[hbm] * 4 + [vmem] + [hbm] * 2 + [vmem] * 6,
        out_specs=[hbm] * 13 + [vmem] * 2,
        out_shape=[
            shape((3, width, columns), B),
            shape((3, 3 * part, columns), B),
            shape((length, width), B),
            shape((length, width), B),
            shape((count, width), B),
            shape((count, width), B),
            shape((count, width), B),
            shape((count, 3 * size), B),
            shape((count, size), B),
            shape((count, hidden), B),
            shape((count, hidden), F),
            shape((half_width, columns), B),
            shape((half_width, columns), F),
            shape((1, 3 * size), F),
            shape((1, width), F),
        ],
        scratch_shapes=[
            pltpu.VMEM((3, width, columns), B),
            pltpu.VMEM((2, CHUNK, width), B),
            pltpu.VMEM((2, CHUNK, width), B),
            pltpu.VMEM((length, width), B),
            pltpu.VMEM((length, width), B),
            pltpu.VMEM((count, width), B),
            pltpu.VMEM((length, width), B),
            pltpu.VMEM((width, columns), F),
            pltpu.VMEM((half_width, columns), B),
            pltpu.VMEM((length, size), B),
            pltpu.VMEM((length, size), B),
            pltpu.VMEM((length, size), B),
            pltpu.VMEM((length, size), B),
            pltpu.VMEM((length, size), B),
            pltpu.VMEM((length, 3 * size), B),
            pltpu.VMEM((length, size), F),
            pltpu.VMEM((length, size), F),
            pltpu.VMEM((2, CHUNK, hidden), B),
            pltpu.VMEM((2, CHUNK, hidden), F),
            pltpu.VMEM((3, part, columns), B),
            pltpu.VMEM((1, length), jnp.int32),
            pltpu.VMEM((length, 8), F),
            pltpu.SemaphoreType.DMA((27,)),
            pltpu.SemaphoreType.DMA((27,)),
            pltpu.SemaphoreType.DMA((3, 6)),
            pltpu.SemaphoreType.DMA((3,)),
            pltpu.SemaphoreType.DMA((3,)),
            pltpu.SemaphoreType.DMA((3, 3)),
            pltpu.SemaphoreType.DMA((2, 2)),
            pltpu.SemaphoreType.DMA((2, 3 + hidden // part)),
            pltpu.SemaphoreType.DMA((2,)),
            pltpu.SemaphoreType.DMA((2, 2)),
            pltpu.SemaphoreType.DMA((2, 5)),
            pltpu.SemaphoreType.DMA((2, 2)),
            pltpu.SemaphoreType.DMA((5,)),
        ],
        compiler_params=pltpu.CompilerParams(
            collective_id=0, has_side_effects=True, vmem_limit_bytes=67043328
        ),
        cost_estimate=pl.CostEstimate(flops=40 * 10**9, bytes_accessed=10**8, transcendentals=10**7),
        name="gather",
    )(
        qkv_weight.reshape(part, 6 * size),
        dense_weight,
        up_weight,
        down_weight,
        segment_ids,
        own_x,
        own_g,
        vectors,
        up_here,
        offsets,
        *tables,
    )
    quarter = length // 4
    tall, blocks = 2 * quarter, width // CHUNK
    dma = pltpu.SemaphoreType.DMA
    block_out, input_grad, qkv_shard, dense_shard, up_shard, down_shard, _, _, _, _, _, _, _, _, small = pl.pallas_call(
        functools.partial(scatter_kernel, groups),
        in_specs=[hbm] * 12 + [vmem] * 3,
        out_specs=[hbm] * 14 + [vmem],
        out_shape=[
            shape((length, width), B),
            shape((length, width), B),
            shape((part, 6 * size), F),
            shape(dense_weight.shape, F),
            shape(up_weight.shape, F),
            shape(down_weight.shape, F),
            shape((3, part, columns), B),
            shape((3, part, columns), B),
            shape((3, half_width, columns), B),
            shape((3, half_width // 2, columns), B),
            shape((3, 3 * part, columns), B),
            shape((2, 2, tall, width), B),
            shape((2, 2, quarter, width), B),
            shape((2, quarter, width), B),
            shape((8, width), F),
        ],
        scratch_shapes=[
            pltpu.VMEM((3, width, columns), B),
            pltpu.VMEM((count, hidden), B),
            pltpu.VMEM((count, hidden), B),
            pltpu.VMEM((tall, width), B),
            pltpu.VMEM((2, count, part), B),
            pltpu.VMEM((2, CHUNK, hidden), F),
            pltpu.VMEM((tall, 3 * size), B),
            pltpu.VMEM((count, size), B),
            pltpu.VMEM((2, half_width, columns), F),
            pltpu.VMEM((half_width, columns), B),
            pltpu.VMEM((2, half_width // 2, columns), B),
            pltpu.VMEM((2, part, columns), B),
            pltpu.VMEM((part, columns), B),
            pltpu.VMEM((tall, width), B),
            pltpu.VMEM((2, tall, CHUNK), B),
            pltpu.VMEM((tall, CHUNK), F),
            pltpu.VMEM((2, 2, quarter, width), B),
            pltpu.VMEM((2, 2, quarter, width), F),
            pltpu.VMEM((tall, 128), F),
            pltpu.VMEM((tall, 128), F),
            pltpu.VMEM((1, hidden), F),
            pltpu.VMEM((8, width), F),
            pltpu.VMEM((5, 8, width), F),
            dma((9,)),
            dma((5, 2)),
            dma((3, 4)),
            dma((3, 4)),
            dma((3, 2)),
            dma((3, 2)),
            dma((3, 3)),
            dma((3, 3)),
            dma((3,)),
            dma((3,)),
            dma((3,)),
            dma((2, 2, blocks)),
            dma((2, 2, blocks)),
            dma((2, 2)),
            dma((2, 2)),
            dma((2,)),
            dma((2,)),
            dma((2, 3)),
            dma((2, 3)),
            dma((3, 2, hidden // part)),
            dma((5,)),
            dma((5,)),
            dma((5,)),
        ],
        compiler_params=pltpu.CompilerParams(
            collective_id=1, has_side_effects=True, vmem_limit_bytes=67043328
        ),
        cost_estimate=pl.CostEstimate(flops=60 * 10**9, bytes_accessed=10**8, transcendentals=10**7),
        name="scatter",
    )(
        attn_send,
        attn_keep,
        weights,
        x_pair,
        g_pair,
        mlp_in,
        mixed_grad,
        context,
        activation,
        slope,
        own_x,
        own_g,
        vectors,
        mixed_sum,
        bias_sum,
    )

    norms, bias_grad, up_bias_grad = small[0:4], small[4], small[5]
    mixed_bias = small[6].reshape(2, width // 2)[:, : 3 * size].reshape(2, 3, size)
    qv_grad = jnp.stack([mixed_bias[:, 0], mixed_bias[:, 2]], axis=1)
    key_bias_grad = mixed_bias[:, 1, :ROT]

    return (
        block_out[None],
        input_grad[None],
        norms[0],
        norms[1],
        norms[2],
        norms[3],
        qkv_shard.reshape(qkv_weight.shape),
        qv_grad,
        key_bias_grad,
        dense_shard,
        bias_grad,
        up_shard,
        up_bias_grad,
        down_shard,
        bias_grad,
    )


def solution(mesh):
    placed = (
        P("dp", None, None),
        P("dp", None),
        P("dp", None, None),
        P(),
        P(),
        P(),
        P(),
        P("dp", "tensor", None, None),
        P("tensor", None, None),
        P("tensor", None),
        P("tensor", None, "dp"),
        P(),
        P("dp", "tensor"),
        P("tensor"),
        P("tensor", "dp"),
        P(),
    )

    def whole(*arrays):
        groups, ways = mesh.shape["dp"], mesh.shape["tensor"]
        part = arrays[0].shape[2] // groups
        chosen = body_narrow if part % 128 or groups != 8 else body
        return chosen(*arrays, groups=groups, ways=ways)

    return jax.shard_map(
        whole,
        mesh=mesh,
        in_specs=placed,
        out_specs=(
            P("dp", None, None),
            P("dp", None, None),
            P(),
            P(),
            P(),
            P(),
            P("dp", "tensor", None, None),
            P("tensor", None, None),
            P("tensor", None),
            P("tensor", None, "dp"),
            P(),
            P("dp", "tensor"),
            P("tensor"),
            P("tensor", "dp"),
            P(),
        ),
        check_vma=False,
    )
```

profile of v0, /device:TPU:0, one launch (start us, length us, event | category | flops | bytes accessed | tf_op | source)
XLA Modules:
  0.0 392.1 jit_solution(17516501252590247572)
XLA Ops:
  0.6 0.0 copy-start.3
  0.7 0.8 constant_dynamic-slice_fusion.1
  1.5 0.1 pad.8.clone
  1.6 0.1 pad.11.clone
  1.7 0.8 constant_dynamic-slice_fusion
  2.4 0.6 copy.37
  3.0 1.3 dynamic_slice.9
  4.3 1.5 stack.36.vec_ref
  5.8 2.0 fusion
  7.8 1.6 maximum_maximum_fusion.2
  9.4 0.0 copy-done.3
  9.4 1.1 copy.33
  10.5 1.6 copy.34.qkv_ref
  12.1 170.6 %gather.1 = (bf16[3,2048,1024]{2,1,0:T(8,128)(2,1)}, bf16[3,768,1024]{2,1,0:T(8,128)(2,1)}, bf16[1024,2048]{1,0:T(8,128)(2,1)}, bf16[1024,2048]{1,0:T(8,128)(2,1...) custom-call(f32[256,1536]{1,0:T(8,128)} %copy.34.qkv_ref, ...), custom_call_target="tpu_custom_call" | custom-call | flops 40000000000 | bytes 100000000 | tf_op jit(solution)/shard_map/gather/pallas_call | solution.py:1766
  182.7 190.5 %scatter.1 = (bf16[1024,2048]{1,0:T(8,128)(2,1)}, bf16[1024,2048]{1,0:T(8,128)(2,1)}, f32[256,1536]{1,0:T(8,128)}, f32[2,256,256]{2,1,0:T(8,128)}, f32[256,2048]...) custom-call(bf16[1024,1024]{1,0:T(8,128)(2,1)} %get-tuple-element.34, ...), custom_call_target="tpu_custom_call" | custom-call | flops 60000002048 | bytes 100000000 | tf_op jit(solution)/shard_map/scatter/pallas_call | solution.py:1845
  373.2 1.8 fusion.3
  375.0 0.0 copy-start.5
  375.1 0.6 slice.60
  375.6 0.6 pad_maximum_fusion
  376.3 1.9 copy.35
  378.1 2.1 copy.36
  380.2 0.6 copy.44
  380.8 4.9 %copy.45 = bf16[1,1024,2048]{2,1,0:T(8,128)(2,1)} copy(bf16[1,1024,2048]{2,1,0:T(8,128)(2,1)} %bitcast.28) | data formatting | bytes 8388608
  385.8 0.0 copy-done.5
  385.8 0.0 copy-done
  385.8 2.1 copy.46
  387.9 0.0 copy-done.4
  387.9 0.8 copy.47
  388.7 0.5 copy-done.2
  389.2 1.3 copy.48
  390.5 0.0 copy-done.1
  390.6 1.3 copy.49
  (14 shorter events, 0.1 us)
Async XLA Ops:
  0.6 8.7 %copy-start.3 = (f32[256,2,3,256]{3,1,2,0:T(2,128)S(1)}, f32[256,2,3,256]{3,1,2,0:T(2,128)}, u32[]{:S(2)}) copy-start(f32[256,2,3,256]{3,1,2,0:T(2,128)} %param.23) | copy-start | bytes 4718596
  375.0 10.7 %copy-start.5 = (f32[1,2048]{1,0:T(1,128)}, f32[1,2048]{1,0:T(1,128)S(1)}, u32[]{:S(2)}) copy-start(f32[1,2048]{1,0:T(1,128)S(1)} %get-tuple-element.86) | copy-start | bytes 24580
  380.8 4.9 %copy-start = (bf16[1024,2048]{1,0:T(8,128)(2,1)S(1)}, bf16[1024,2048]{1,0:T(8,128)(2,1)}, u32[]{:S(2)}) copy-start(bf16[1024,2048]{1,0:T(8,128)(2,1)} %get-tuple-element.47) | copy-start | bytes 12582916
  385.8 2.1 copy-start.4
  385.8 3.5 copy-start.2
  387.9 2.6 copy-start.1
where the time goes:
time: 398 us; the launch traced here: 392 us
  Pallas kernels  361 us (91%)
  local copies, waits for them, and re-layouts  25.8 us (6%)
  other arithmetic  4.18 us (1%)
    pallas_call x1, Pallas kernels, body(): pl.pallas_call(functools.partial(scatter_kernel, groups), in_specs=[hbm]...  190 us
    pallas_call x1, Pallas kernels, body(): pl.pallas_call(functools.partial(gather_kernel, groups), in_specs=[hbm] *...  171 us
    unnamed x21, local copies, waits for them, and re-layouts  15.4 us

commit v1 on v0

--- a/solution.py
+++ b/solution.py
@@ -151,80 +151,139 @@
     pl.semaphore_wait(barrier, len(partners))
 
 
-GATHERING = (
+STEPS_ONE = (
     ("x1", "i"),
+    ("sh", 0, 0),
     ("sh", 0, 1),
+    ("pu", 0, "o"),
     ("pu", 0, "i"),
-    ("pu", 0, "o"),
+    ("sh", 1, 1),
+    ("yo", 0, 0),
+    ("gst", 0),
+    ("sh", 1, 0),
+    ("hd", 0, "o"),
+    ("x1", "o"),
+    ("yo", 0, 1),
+    ("re", 0),
+    ("hd", 0, "i"),
+    ("gst", 1),
     ("sh", 2, 0),
-    ("sh", 0, 0),
-    ("hd", 0, "o"),
+    ("gpo", 0, 2),
+    ("gpo", 0, 0),
+    ("pu", 1, "o"),
+    ("pu", 1, "i"),
+    ("sh", 2, 1),
+    ("yo", 0, 3),
+    ("x2",),
     ("yo", 2, 0),
-    ("yo", 0, 0),
-    ("hd", 0, "i"),
-    ("st", 0),
-    ("x1", "o"),
-    ("sh", 1, 1),
-    ("sh", 1, 0),
-    ("sh", 2, 1),
-    ("po", 0, 0),
-    ("pu", 1, "o"),
     ("N", 0),
-    ("re", 0),
-    ("pu", 1, "i"),
+    ("g1", "o"),
+    ("gpo", 0, 1),
+    ("yo", 0, 2),
+    ("yo", 1, 0),
     ("hd", 1, "i"),
-    ("yo", 1, 0),
-    ("yo", 0, 1),
-    ("st", 1),
+    ("yo", 1, 1),
+    ("g1", "i"),
+    ("hd", 2, "o"),
+    ("G", 0),
+    ("re", 1),
+    ("x3",),
+    ("hd", 2, "i"),
     ("hd", 1, "o"),
-    ("po", 0, 1),
-    ("g1", "o"),
-    ("G", 0),
-    ("x2",),
-    ("yo", 0, 2),
-    ("yo", 0, 3),
-    ("po", 0, 2),
-    ("g1", "i"),
-    ("po", 1, 1),
-    ("po", 1, 0),
+    ("PJ", 0),
+    ("CG", 0),
+    ("g2",),
     ("pu", 2, "o"),
-    ("PJ", 0),
-    ("re", 1),
-    ("CG", 0),
-    ("hd", 2, "o"),
+    ("AT", 0),
+    ("gpo", 1, 2),
+    ("GR", 0, 0),
+    ("gpo", 2, 0),
+    ("yo", 1, 3),
     ("pu", 2, "i"),
-    ("hd", 2, "i"),
-    ("yo", 1, 1),
-    ("AT", 0),
-    ("g2",),
-    ("GR", 0, 0),
-    ("po", 1, 2),
-    ("x3",),
-    ("yo", 1, 2),
+    ("gpo", 1, 0),
+    ("gpo", 1, 1),
     ("GR", 0, 1),
     ("N", 1),
     ("yo", 2, 1),
+    ("g3",),
+    ("gpo", 2, 1),
     ("re", 2),
-    ("po", 2, 1),
+    ("gst", 2),
     ("PJ", 1),
-    ("po", 2, 0),
-    ("g3",),
-    ("yo", 1, 3),
     ("G", 1),
     ("CG", 1),
-    ("st", 2),
+    ("yo", 1, 2),
     ("AT", 1),
+    ("gpo", 2, 2),
+    ("GR", 1, 0),
     ("yo", 2, 2),
-    ("po", 2, 2),
-    ("GR", 1, 0),
+    ("GR", 1, 1),
     ("UP", 0),
     ("yo", 2, 3),
     ("UP", 1),
-    ("GR", 1, 1),
 )
 
-
-def gather_kernel(
+STEPS_TWO = (
+    ("ps", 2),
+    ("st", 1, 1),
+    ("pre", 1),
+    ("yf", 0, 3),
+    ("kt", 1, 1),
+    ("pk", 2),
+    ("po", 0, 1),
+    ("yf", 0, 2),
+    ("st", 0, 1),
+    ("yn", 0, 1),
+    ("kt", 0, 1),
+    ("es", 1),
+    ("st", 1, 0),
+    ("po", 0, 0),
+    ("pre", 0),
+    ("yf", 2, 3),
+    ("yn", 0, 0),
+    ("zl", 0, 1),
+    ("kt", 1, 0),
+    ("yf", 2, 2),
+    ("po", 0, 2),
+    ("st", 0, 0),
+    ("kt", 0, 0),
+    ("po", 2, 1),
+    ("sb",),
+    ("es", 0),
+    ("ps", 1),
+    ("se", 0),
+    ("zl", 0, 0),
+    ("fin", 1),
+    ("po", 2, 0),
+    ("pk", 1),
+    ("yf", 1, 3),
+    ("po", 2, 2),
+    ("fin", 0),
+    ("fa", 0),
+    ("yf", 1, 2),
+    ("yn", 2, 0),
+    ("yn", 2, 1),
+    ("zl", 2, 1),
+    ("se", 1),
+    ("po", 1, 1),
+    ("po", 1, 2),
+    ("po", 1, 0),
+    ("fe", 1),
+    ("se", 2),
+    ("yn", 1, 1),
+    ("yn", 1, 0),
+    ("zl", 1, 1),
+    ("fe", 0),
+    ("se", 3),
+    ("zl", 1, 0),
+    ("fa", 2),
+    ("zl", 2, 0),
+    ("se", 4),
+    ("fa", 1),
+)
+
+
+def gather_steps(
     groups,
     qkv_ref,
     dense_ref,
@@ -236,10 +295,7 @@
     vec_ref,
     up_bias_ref,
     offset_ref,
-    cos_ref,
-    above_ref,
-    below_ref,
-    w_out,
+    tables_ref,
     w_relay,
     x_other,
     g_other,
@@ -252,30 +308,11 @@
     slope_out,
     send_out,
     keep_out,
+    w,
+    theirs_v,
+    seg_v,
     sum_ref,
     bias_ref,
-    w,
-    raw_x,
-    raw_g,
-    attn_v,
-    g_v,
-    mlp_v,
-    xr_v,
-    grad_v,
-    send_v,
-    q_v,
-    k_v,
-    v_v,
-    cg_v,
-    ctx_v,
-    mg_v,
-    dk_v,
-    dv_v,
-    act_v,
-    slope_v,
-    theirs_v,
-    seg_v,
-    col_v,
     send_sem,
     recv_sem,
     cross_sem,
@@ -292,14 +329,15 @@
 ):
     length, width = x_ref.shape
     part = width // groups
-    size = q_v.shape[1]
+    size = dense_ref.shape[1]
     quarter = length // 4
     me, place = lax.axis_index("dp"), lax.axis_index("tensor")
     core, side = lax.rem(place, 2), lax.div(place, 2)
     pair_to, side_to, core_to = flip(me, PAIR), flip(place, 2), flip(place, 1)
     spread, order = block_order(groups)
     half = bit_of(me, PAIR)
-    hidden = slope_v.shape[2]
+    hidden = act_out.shape[1]
+    raw_x = attn_v = g_v = mlp_v = xr_v = grad_v = send_v = q_v = k_v = v_v = cg_v = ctx_v = mg_v = dk_v = dv_v = act_v = slope_v = col_v = tab_v = None
 
     def shards(owner, slot):
         at = pl.ds(pl.multiple_of(owner * 3 * size, 128), 3 * size)
@@ -319,10 +357,7 @@
             for number, (source, target) in enumerate(spots)
         ]
 
-    shard_copies = [shards(half, 0), shards(1 - half, 1)]
-    for number in range(3 + hidden // part):
-        for slot in (1, 0):
-            shard_copies[slot][number].start()
+    shard_copies = []
 
     def shard(group, slot):
         for copy in shard_copies[slot][(0, 2, 3)[group] : (2, 3, None)[group]]:
@@ -346,14 +381,10 @@
 
     across = PAIR | spread[0]
     inner = bit_of(me, PAIR) != bit_of(me, spread[0])
-    greet(
-        [("dp", flip(me, mask)) for mask in [PAIR, across] + spread] + [("tensor", side_to), ("tensor", core_to)]
-    )
     outer = bit_of(me, PAIR) == bit_of(me, spread[0])
-    copies, partial_copies = {}, []
-
-    def remote(key, source, target, axis, index):
-        number = len(copies)
+    copies = {}
+
+    def remote(key, number, source, target, axis, index):
         copies[key] = pltpu.make_async_remote_copy(
             src_ref=source,
             dst_ref=target,
@@ -367,27 +398,21 @@
     def rows(position):
         return pl.ds(position * part, part)
 
-    def pair_up(group, here=None):
-        key = ("w", group, 1)
-        if key not in copies:
-            number = len(copies)
-            copies[key] = pltpu.make_async_remote_copy(
-                src_ref=theirs_v.at[group],
-                dst_ref=w.at[group, rows(1)],
-                send_sem=send_sem.at[number],
-                recv_sem=recv_sem.at[number],
-                device_id={"dp": pair_to},
-                device_id_type=MESH,
-            )
-        if here is None:
-            copies[key].start()
-        else:
-            pl.when(here)(copies[key].start)
+    def pair_up(group, here):
+        copy = pltpu.make_async_remote_copy(
+            src_ref=theirs_v.at[group],
+            dst_ref=w.at[group, rows(1)],
+            send_sem=send_sem.at[8 * group + 1],
+            recv_sem=recv_sem.at[8 * group + 1],
+            device_id={"dp": pair_to},
+            device_id_type=MESH,
+        )
+        pl.when(here)(copy.start)
 
     def onward(group, position, level):
         source = w.at[group, rows(position)]
         far = position + (2 << level)
-        remote(("w", group, far), source, w.at[group, rows(far)], "dp", flip(me, spread[level]))
+        remote(("w", far), 8 * group + far, source, w.at[group, rows(far)], "dp", flip(me, spread[level]))
 
     def partly(here, source, target, send, recv, to):
         copy = pltpu.make_async_remote_copy(
@@ -398,17 +423,12 @@
             device_id={"dp": to},
             device_id_type=MESH,
         )
-        partial_copies.append((here, copy))
         pl.when(here)(copy.start)
-        return copy
 
     across_to = flip(me, across)
 
     def straight(group):
-        copy = partly(
-            inner, theirs_v.at[group], w.at[group, rows(3)], cross_sem.at[group, 0], three_sem.at[group], across_to
-        )
-        copies[("w", group, 3)] = copy
+        partly(inner, theirs_v.at[group], w.at[group, rows(3)], cross_sem.at[group, 0], three_sem.at[group], across_to)
 
     def hand(group, here=None):
         source, sem = w.at[group, rows(0)], cross_sem.at[group, 1]
@@ -435,7 +455,7 @@
                 device_id_type=MESH,
             )
             pl.when(inner)(here.wait_recv)
-            copy = partly(
+            partly(
                 inner,
                 source,
                 w.at[group, rows(target)],
@@ -443,7 +463,6 @@
                 (three_sem if target == 3 else two_sem).at[group],
                 across_to if number == 0 else pair_to,
             )
-            copies[("w", group, target)] = copy
 
     def to_pair(key, source, target, here):
         if key not in quarters:
@@ -455,7 +474,6 @@
                 device_id={"dp": pair_to},
                 device_id_type=MESH,
             )
-            partial_copies.append((None, quarters[key]))
         pl.when(here)(quarters[key].start)
 
     quarters = {}
@@ -464,7 +482,15 @@
     def arrive(group, position):
         if (group, position) not in arrived:
             arrived.add((group, position))
-            copies[("w", group, position)].wait_recv()
+            sem = {2: two_sem.at[group], 3: three_sem.at[group]}.get(position, recv_sem.at[8 * group + position])
+            pltpu.make_async_remote_copy(
+                src_ref=w.at[group, rows(position)],
+                dst_ref=w.at[group, rows(position)],
+                send_sem=sem,
+                recv_sem=sem,
+                device_id={"dp": pair_to},
+                device_id_type=MESH,
+            ).wait_recv()
 
     spot = pl.ds(pl.multiple_of(core * (2 * quarter) + side * quarter, quarter), quarter)
     pair_rows = pl.ds(pl.multiple_of(core * (2 * quarter), quarter), 2 * quarter)
@@ -534,29 +560,30 @@
         def work(tile, slot):
             here = pl.ds(pl.multiple_of(tile * CHUNK, CHUNK), CHUNK)
             if seq == 0:
-                bias_ref[...] += jnp.sum(raw_g[slot].astype(F), axis=0, keepdims=True)
+                bias_ref[...] += jnp.sum(raw_x[slot].astype(F), axis=0, keepdims=True)
             for position, mask in enumerate(order):
                 to = slice(position * part, (position + 1) * part)
                 there = pl.ds(pl.multiple_of(flip(me, mask) * part, part), part)
-                g_v[here, to] = raw_g[slot, :, there]
-
-        over_tiles(g_other if seq else g_ref, raw_g, 1, work)
+                g_v[here, to] = raw_x[slot, :, there]
+
+        over_tiles(g_other if seq else g_ref, raw_x, 1, work)
         leave(("g", seq), g_v, g_rel.at[pl.ds(seq * length, length)], rel_sem.at[seq, 1])
 
     def whole_group(group):
         if ("out", group) not in arrived:
             arrived.add(("out", group))
-            for position in range(4, 8):
+            for position in range(1, 8):
                 arrive(group, position)
-            leave(("w", group), w.at[group], w_out.at[group], out_sem.at[group])
 
     def project(seq):
         whole_group(0)
+        if seq == 0:
+            left("tables")
 
         def one(tile, carry):
             here = pl.ds(pl.multiple_of(tile * CHUNK, CHUNK), CHUNK)
             mixed = dot(attn_v[here], w[0, :, : 3 * size], ((1,), (0,)), F) + offset_ref[...]
-            tables = (cos_ref[here], above_ref[here], below_ref[here])
+            tables = (tab_v[0, here], tab_v[1, here], tab_v[2, here])
             q_v[here] = turn(mixed[:, :size], *tables).astype(B)
             k_v[here] = turn(mixed[:, size : 2 * size], *tables).astype(B)
             v_v[here] = mixed[:, 2 * size :].astype(B)
@@ -570,7 +597,7 @@
 
     def attend(seq):
         if seq:
-            seg_copy.wait()
+            copies["seg"].wait()
             left(("mg", 0), ("ctx", 0))
         scale = size ** (-0.5)
         ids = seg_ref[...] if seq == 0 else seg_v[...]
@@ -595,12 +622,12 @@
             centred = jnp.sum(probs * prob_grad, axis=1, keepdims=True)
             score_grad = (probs * (prob_grad - centred)).astype(B)
             q_grad = dot(score_grad, k_v[keys], ((1,), (0,)), F) * scale
-            tables = (cos_ref[here], -above_ref[here], -below_ref[here])
+            tables = (tab_v[0, here], -tab_v[1, here], -tab_v[2, here])
             mg_v[here, :size] = turn(q_grad, *tables).astype(B)
             dk_v[keys] += dot(score_grad, q_v[here], ((0,), (0,)), F) * scale
         for first in range(0, length, QBLOCK):
             here = slice(first, first + QBLOCK)
-            tables = (cos_ref[here], -above_ref[here], -below_ref[here])
+            tables = (tab_v[0, here], -tab_v[1, here], -tab_v[2, here])
             mg_v[here, size : 2 * size] = turn(dk_v[here], *tables).astype(B)
             mg_v[here, 2 * size :] = dv_v[here].astype(B)
         sums = jnp.sum(mg_v[...].astype(F), axis=0, keepdims=True)
@@ -658,15 +685,6 @@
             for copy in store(tile, tile % 2):
                 copy.wait()
 
-    seg_copy = pltpu.make_async_remote_copy(
-        src_ref=seg_ref,
-        dst_ref=seg_v,
-        send_sem=seg_sem.at[0],
-        recv_sem=seg_sem.at[1],
-        device_id={"dp": pair_to},
-        device_id_type=MESH,
-    )
-    seg_copy.start()
     kinds = {"o": outer, "i": inner}
 
     def relay_on(group):
@@ -680,11 +698,11 @@
 
     def to_side(name, number, array):
         quarters[number].wait_recv()
-        remote(name + "2", array.at[spot], array.at[spot], "tensor", side_to)
+        remote(name + "2", 24 + number, array.at[spot], array.at[spot], "tensor", side_to)
 
     def to_core(name, array):
         copies[name + "2"].wait_recv()
-        remote(name + "3", array.at[pair_rows], array.at[pair_rows], "tensor", core_to)
+        remote(name + "3", 26 + (name == "g"), array.at[pair_rows], array.at[pair_rows], "tensor", core_to)
 
     def gradients(seq, number):
         middle = width // 2
@@ -702,11 +720,11 @@
     stages = {
         "sh": shard,
         "pu": lambda group, kind: pair_up(group, kinds[kind]),
-        "st": straight,
+        "gst": straight,
         "hd": lambda group, kind: hand(group, kinds[kind]),
         "re": relay_on,
         "yo": send_y,
-        "po": pass_on,
+        "gpo": pass_on,
         "x1": lambda kind: to_pair(0, x_ref.at[spot], x_other.at[spot], kinds[kind]),
         "g1": lambda kind: to_pair(1, g_ref.at[spot], g_other.at[spot], kinds[kind]),
         "x2": lambda: to_side("x", 0, x_other),
@@ -721,84 +739,86 @@
         "GR": gradients,
         "UP": lift,
     }
-    for name, *numbers in GATHERING:
-        stages[name](*numbers)
-    whole_group(2)
-    left(*list(outs))
-    for key, copy in copies.items():
-        if key[0] != "w" or key[2] not in (2, 3):
-            copy.wait_send()
-    for here, copy in partial_copies:
-        if here is None:
-            copy.wait_send()
-        else:
-            pl.when(here)(copy.wait_send)
-
-
-SCHEDULE = (
-    ("pre", 1),
-    ("st", 1, 1),
-    ("yf", 0, 3),
-    ("kt", 1, 1),
-    ("ps", 2),
-    ("yf", 0, 2),
-    ("st", 0, 1),
-    ("yn", 0, 1),
-    ("kt", 0, 1),
-    ("po", 0, 1),
-    ("es", 1),
-    ("st", 1, 0),
-    ("po", 0, 2),
-    ("po", 0, 0),
-    ("pk", 2),
-    ("kt", 1, 0),
-    ("pre", 0),
-    ("yf", 2, 3),
-    ("st", 0, 0),
-    ("yn", 0, 0),
-    ("yf", 2, 2),
-    ("kt", 0, 0),
-    ("sb",),
-    ("es", 0),
-    ("po", 2, 1),
-    ("ps", 1),
-    ("se", 0),
-    ("zl", 0, 1),
-    ("zl", 0, 0),
-    ("po", 2, 0),
-    ("pk", 1),
-    ("yf", 1, 3),
-    ("fin", 1),
-    ("yn", 2, 0),
-    ("se", 1),
-    ("yf", 1, 2),
-    ("yn", 2, 1),
-    ("po", 2, 2),
-    ("zl", 2, 1),
-    ("fin", 0),
-    ("fa", 0),
-    ("po", 1, 1),
-    ("yn", 1, 0),
-    ("po", 1, 2),
-    ("yn", 1, 1),
-    ("po", 1, 0),
-    ("se", 2),
-    ("zl", 1, 1),
-    ("zl", 1, 0),
-    ("fa", 2),
-    ("fe", 1),
-    ("fe", 0),
-    ("zl", 2, 0),
-    ("se", 3),
-    ("se", 4),
-    ("fa", 1),
-)
-
-def scatter_kernel(
+    def begin(*private):
+        nonlocal raw_x, attn_v, g_v, mlp_v, xr_v, grad_v, send_v, q_v, k_v
+        nonlocal v_v, cg_v, ctx_v, mg_v, dk_v, dv_v, act_v, slope_v, col_v, tab_v
+        (
+            raw_x,
+            attn_v,
+            g_v,
+            mlp_v,
+            xr_v,
+            grad_v,
+            send_v,
+            q_v,
+            k_v,
+            v_v,
+            cg_v,
+            ctx_v,
+            mg_v,
+            dk_v,
+            dv_v,
+            act_v,
+            slope_v,
+            col_v,
+            tab_v,
+        ) = private
+        shard_copies.extend([shards(half, 0), shards(1 - half, 1)])
+        for number in range(3 + hidden // part):
+            for slot in (1, 0):
+                shard_copies[slot][number].start()
+        leave("tables", tables_ref, tab_v, out_sem.at[0])
+        greet(
+            [("dp", flip(me, mask)) for mask in [PAIR, across] + spread] + [("tensor", side_to), ("tensor", core_to)]
+        )
+        copies["seg"] = pltpu.make_async_remote_copy(
+            src_ref=seg_ref,
+            dst_ref=seg_v,
+            send_sem=seg_sem.at[0],
+            recv_sem=seg_sem.at[1],
+            device_id={"dp": pair_to},
+            device_id_type=MESH,
+        )
+        copies["seg"].start()
+
+    def close():
+        left(*list(outs))
+        for name in ("x2", "x3", "g2", "g3"):
+            copies[name].wait_send()
+        for key in (0, 1):
+            quarters[key].wait_send()
+
+    def finish():
+        def gone(sem):
+            pltpu.make_async_remote_copy(
+                src_ref=w.at[0, rows(0)],
+                dst_ref=w.at[0, rows(0)],
+                send_sem=sem,
+                recv_sem=sem,
+                device_id={"dp": pair_to},
+                device_id_type=MESH,
+            ).wait_send()
+
+        for group in range(3):
+            for position in (1, 4, 5, 6, 7):
+                gone(send_sem.at[8 * group + position])
+            gone(cross_sem.at[group, 1])
+
+            @pl.when(inner)
+            def _():
+                for number in (0, 2, 3, 4, 5):
+                    gone(cross_sem.at[group, number])
+
+    return begin, stages, whole_group, close, finish
+
+
+def scatter_steps(
     groups,
+    steps,
+    earlier,
+    whole_group,
     attn_send,
     attn_keep,
-    weights,
     x_rel,
     g_rel,
     mlp_in,
@@ -827,27 +847,6 @@
     e_recv,
     small_out,
     w,
-    act_v,
-    pre_v,
-    tile_v,
-    col_v,
-    slope_t,
-    mix_t,
-    ctx_v,
-    keep_v,
-    y_send,
-    z_send,
-    p_send,
-    y_stage,
-    c_send,
-    c_stage,
-    r_stage,
-    x_send,
-    hold_v,
-    mean_v,
-    inverse_v,
-    sum_v,
-    small_v,
     small_recv,
     load_sem,
     tile_sem,
@@ -872,6 +871,27 @@
     ss_sem,
     sr_sem,
     out_sem,
+    act_v,
+    pre_v,
+    tile_v,
+    col_v,
+    slope_t,
+    mix_t,
+    ctx_v,
+    keep_v,
+    y_send,
+    z_send,
+    p_send,
+    y_stage,
+    c_send,
+    c_stage,
+    r_stage,
+    x_send,
+    hold_v,
+    mean_v,
+    inverse_v,
+    sum_v,
+    small_v,
 ):
     length, width = x_ref.shape
     part = width // groups
@@ -886,7 +906,6 @@
     across_to = flip(z_to, PAIR)
     inner = bit_of(me, PAIR) != bit_of(me, spread[0])
     outer = bit_of(me, PAIR) == bit_of(me, spread[0])
-    greet([("dp", to) for to in (pair_to, z_to, y_to, across_to)] + [("tensor", side_to), ("tensor", core_to)])
 
     def remote(source, target, send, recv, axis, index):
         return pltpu.make_async_remote_copy(
@@ -1057,14 +1076,14 @@
             emit_near(group)
 
     loads = [
-        pltpu.make_async_copy(weights.at[2], w.at[2], load_sem.at[0]),
-        pltpu.make_async_copy(weights.at[0], w.at[0], load_sem.at[1]),
-        pltpu.make_async_copy(weights.at[1], w.at[1], load_sem.at[2]),
+        None,
+        None,
+        None,
         pltpu.make_async_copy(activation, act_v, load_sem.at[3]),
         pltpu.make_async_copy(context, ctx_v, load_sem.at[4]),
         pltpu.make_async_copy(attn_keep, keep_v.at[0], load_sem.at[5]),
     ]
-    for number in (4, 3, 1, 0, 5, 2):
+    for number in (3, 5, 4):
         loads[number].start()
     loaded = set()
 
@@ -1089,7 +1108,7 @@
     sum_v[...] = jnp.zeros_like(sum_v)
 
     def pre_tiles(seq):
-        need(0)
+        whole_group(2)
         low, high = seq * length // CHUNK, (seq + 1) * length // CHUNK
         for copy in pre_load(low, 0):
             copy.start()
@@ -1137,7 +1156,9 @@
 
     def send_tile(which, seq):
         begin, block_of = tile_of[which]
-        need(*((1, 2) if which == 0 else (0, 1, 3, 4)))
+        whole_group(2)
+        if which:
+            need(3, 4)
         start = pl.multiple_of(seq * length + (1 - core) * tall, tall)
         begin(start)
 
@@ -1426,8 +1447,8 @@
         "sb": small_begin,
         "se": small_end,
     }
-    for name, *numbers in SCHEDULE:
-        stages[name](*numbers)
+    for name, *numbers in steps:
+        (stages if name in stages else earlier)[name](*numbers)
     small_out[...] = small_v[...]
     for end in ends:
         end()
@@ -1453,6 +1474,210 @@
         e_copy(which).wait_send()
         if which:
             x_copy(which, 0).wait_send()
+
+
+def layer_kernel(
+    groups,
+    scoped_one,
+    scoped_two,
+    qkv_ref,
+    dense_ref,
+    up_ref,
+    down_ref,
+    seg_ref,
+    x_ref,
+    g_ref,
+    vec_ref,
+    up_bias_ref,
+    offset_ref,
+    tables_ref,
+    block_out,
+    input_grad,
+    qkv_out,
+    dense_out,
+    up_out,
+    down_out,
+    w_relay,
+    x_other,
+    g_other,
+    x_rel,
+    g_rel,
+    mlp_out,
+    mixed_out,
+    ctx_out,
+    act_out,
+    slope_out,
+    send_out,
+    keep_out,
+    far_in,
+    far_two,
+    y_recv,
+    z_recv,
+    z_relay,
+    c_recv,
+    x_recv,
+    e_recv,
+    small_out,
+    w,
+    theirs_v,
+    seg_v,
+    sum_ref,
+    bias_ref,
+    small_recv,
+    send_sem,
+    recv_sem,
+    cross_sem,
+    two_sem,
+    three_sem,
+    relay_sem,
+    quarter_sem,
+    shard_sem,
+    seg_sem,
+    load_sem,
+    rel_sem,
+    tile_sem,
+    out_sem,
+    s_load_sem,
+    s_tile_sem,
+    s_ys_sem,
+    s_yr_sem,
+    s_zs_sem,
+    s_zr_sem,
+    s_zl_sem,
+    s_zf_sem,
+    s_two_sem,
+    s_ps_sem,
+    s_pr_sem,
+    s_cs_sem,
+    s_cr_sem,
+    s_xs_sem,
+    s_xr_sem,
+    s_es_sem,
+    s_er_sem,
+    s_fs_sem,
+    s_fr_sem,
+    s_emit_sem,
+    s_ss_sem,
+    s_sr_sem,
+    s_out_sem,
+):
+    begin, earlier, whole_group, close, finish = gather_steps(
+        groups,
+        qkv_ref,
+        dense_ref,
+        up_ref,
+        down_ref,
+        seg_ref,
+        x_ref,
+        g_ref,
+        vec_ref,
+        up_bias_ref,
+        offset_ref,
+        tables_ref,
+        w_relay,
+        x_other,
+        g_other,
+        x_rel,
+        g_rel,
+        mlp_out,
+        mixed_out,
+        ctx_out,
+        act_out,
+        slope_out,
+        send_out,
+        keep_out,
+        w,
+        theirs_v,
+        seg_v,
+        sum_ref,
+        bias_ref,
+        send_sem,
+        recv_sem,
+        cross_sem,
+        two_sem,
+        three_sem,
+        relay_sem,
+        quarter_sem,
+        shard_sem,
+        seg_sem,
+        load_sem,
+        rel_sem,
+        tile_sem,
+        out_sem,
+    )
+
+    def first(*private):
+        begin(*private)
+        for name, *numbers in STEPS_ONE:
+            earlier[name](*numbers)
+        close()
+
+    def second(*private):
+        scatter_steps(
+            groups,
+            STEPS_TWO,
+            earlier,
+            whole_group,
+            send_out,
+            keep_out,
+            x_rel,
+            g_rel,
+            mlp_out,
+            mixed_out,
+            ctx_out,
+            act_out,
+            slope_out,
+            x_ref,
+            g_ref,
+            vec_ref,
+            sum_ref,
+            bias_ref,
+            block_out,
+            input_grad,
+            qkv_out,
+            dense_out,
+            up_out,
+            down_out,
+            far_in,
+            far_two,
+            y_recv,
+            z_recv,
+            z_relay,
+            c_recv,
+            x_recv,
+            e_recv,
+            small_out,
+            w,
+            small_recv,
+            s_load_sem,
+            s_tile_sem,
+            s_ys_sem,
+            s_yr_sem,
+            s_zs_sem,
+            s_zr_sem,
+            s_zl_sem,
+            s_zf_sem,
+            s_two_sem,
+            s_ps_sem,
+            s_pr_sem,
+            s_cs_sem,
+            s_cr_sem,
+            s_xs_sem,
+            s_xr_sem,
+            s_es_sem,
+            s_er_sem,
+            s_fs_sem,
+            s_fr_sem,
+            s_emit_sem,
+            s_ss_sem,
+            s_sr_sem,
+            s_out_sem,
+            *private,
+        )
+        finish()
+
+    pl.run_scoped(first, *scoped_one)
+    pl.run_scoped(second, *scoped_two)
 
 
 def body_narrow(
@@ -1747,28 +1972,64 @@
     columns = hidden
     half_width = width // 2
     vmem, hbm = pl.BlockSpec(memory_space=pltpu.VMEM), pl.BlockSpec(memory_space=pl.ANY)
-    (
-        weights,
-        _,
-        _,
-        _,
-        x_pair,
-        g_pair,
-        mlp_in,
-        mixed_grad,
-        context,
-        activation,
-        slope,
-        attn_send,
-        attn_keep,
-        mixed_sum,
-        bias_sum,
-    ) = pl.pallas_call(
-        functools.partial(gather_kernel, groups),
-        in_specs=[hbm] * 4 + [vmem] + [hbm] * 2 + [vmem] * 6,
-        out_specs=[hbm] * 13 + [vmem] * 2,
+    quarter = length // 4
+    tall, blocks = 2 * quarter, width // CHUNK
+    dma = pltpu.SemaphoreType.DMA
+    scoped_one = [
+        pltpu.VMEM((2, CHUNK, width), B),
+        pltpu.VMEM((length, width), B),
+        pltpu.VMEM((length, width), B),
+        pltpu.VMEM((count, width), B),
+        pltpu.VMEM((length, width), B),
+        pltpu.VMEM((width, columns), F),
+        pltpu.VMEM((half_width, columns), B),
+        pltpu.VMEM((length, size), B),
+        pltpu.VMEM((length, size), B),
+        pltpu.VMEM((length, size), B),
+        pltpu.VMEM((length, size), B),
+        pltpu.VMEM((length, size), B),
+        pltpu.VMEM((length, 3 * size), B),
+        pltpu.VMEM((length, size), F),
+        pltpu.VMEM((length, size), F),
+        pltpu.VMEM((2, CHUNK, hidden), B),
+        pltpu.VMEM((2, CHUNK, hidden), F),
+        pltpu.VMEM((length, 8), F),
+        pltpu.VMEM((3, length, 128), F),
+    ]
+    scoped_two = [
+        pltpu.VMEM((count, hidden), B),
+        pltpu.VMEM((count, hidden), B),
+        pltpu.VMEM((tall, width), B),
+        pltpu.VMEM((2, count, part), B),
+        pltpu.VMEM((2, CHUNK, hidden), F),
+        pltpu.VMEM((tall, 3 * size), B),
+        pltpu.VMEM((count, size), B),
+        pltpu.VMEM((2, half_width, columns), F),
+        pltpu.VMEM((half_width, columns), B),
+        pltpu.VMEM((2, half_width // 2, columns), B),
+        pltpu.VMEM((2, part, columns), B),
+        pltpu.VMEM((part, columns), B),
+        pltpu.VMEM((tall, width), B),
+        pltpu.VMEM((2, tall, CHUNK), B),
+        pltpu.VMEM((tall, CHUNK), F),
+        pltpu.VMEM((2, 2, quarter, width), B),
+        pltpu.VMEM((2, 2, quarter, width), F),
+        pltpu.VMEM((tall, 128), F),
+        pltpu.VMEM((tall, 128), F),
+        pltpu.VMEM((1, hidden), F),
+        pltpu.VMEM((8, width), F),
+    ]
+    block_out, input_grad, qkv_shard, dense_shard, up_shard, down_shard, *_, small = pl.pallas_call(
+        functools.partial(layer_kernel, groups, scoped_one, scoped_two),
+        in_specs=[hbm] * 4 + [vmem] + [hbm] * 2 + [vmem] * 3 + [hbm],
+        out_specs=[hbm] * 26 + [vmem],
         out_shape=[
-            shape((3, width, columns), B),
+            shape((length, width), B),
+            shape((length, width), B),
+            shape((part, 6 * size), F),
+            shape(dense_weight.shape, F),
+            shape(up_weight.shape, F),
+            shape(down_weight.shape, F),
             shape((3, 3 * part, columns), B),
             shape((length, width), B),
             shape((length, width), B),
@@ -1781,78 +2042,6 @@
             shape((count, hidden), F),
             shape((half_width, columns), B),
             shape((half_width, columns), F),
-            shape((1, 3 * size), F),
-            shape((1, width), F),
-        ],
-        scratch_shapes=[
-            pltpu.VMEM((3, width, columns), B),
-            pltpu.VMEM((2, CHUNK, width), B),
-            pltpu.VMEM((2, CHUNK, width), B),
-            pltpu.VMEM((length, width), B),
-            pltpu.VMEM((length, width), B),
-            pltpu.VMEM((count, width), B),
-            pltpu.VMEM((length, width), B),
-            pltpu.VMEM((width, columns), F),
-            pltpu.VMEM((half_width, columns), B),
-            pltpu.VMEM((length, size), B),
-            pltpu.VMEM((length, size), B),
-            pltpu.VMEM((length, size), B),
-            pltpu.VMEM((length, size), B),
-            pltpu.VMEM((length, size), B),
-            pltpu.VMEM((length, 3 * size), B),
-            pltpu.VMEM((length, size), F),
-            pltpu.VMEM((length, size), F),
-            pltpu.VMEM((2, CHUNK, hidden), B),
-            pltpu.VMEM((2, CHUNK, hidden), F),
-            pltpu.VMEM((3, part, columns), B),
-            pltpu.VMEM((1, length), jnp.int32),
-            pltpu.VMEM((length, 8), F),
-            pltpu.SemaphoreType.DMA((27,)),
-            pltpu.SemaphoreType.DMA((27,)),
-            pltpu.SemaphoreType.DMA((3, 6)),
-            pltpu.SemaphoreType.DMA((3,)),
-            pltpu.SemaphoreType.DMA((3,)),
-            pltpu.SemaphoreType.DMA((3, 3)),
-            pltpu.SemaphoreType.DMA((2, 2)),
-            pltpu.SemaphoreType.DMA((2, 3 + hidden // part)),
-            pltpu.SemaphoreType.DMA((2,)),
-            pltpu.SemaphoreType.DMA((2, 2)),
-            pltpu.SemaphoreType.DMA((2, 5)),
-            pltpu.SemaphoreType.DMA((2, 2)),
-            pltpu.SemaphoreType.DMA((5,)),
-        ],
-        compiler_params=pltpu.CompilerParams(
-            collective_id=0, has_side_effects=True, vmem_limit_bytes=67043328
-        ),
-        cost_estimate=pl.CostEstimate(flops=40 * 10**9, bytes_accessed=10**8, transcendentals=10**7),
-        name="gather",
-    )(
-        qkv_weight.reshape(part, 6 * size),
-        dense_weight,
-        up_weight,
-        down_weight,
-        segment_ids,
-        own_x,
-        own_g,
-        vectors,
-        up_here,
-        offsets,
-        *tables,
-    )
-    quarter = length // 4
-    tall, blocks = 2 * quarter, width // CHUNK
-    dma = pltpu.SemaphoreType.DMA
-    block_out, input_grad, qkv_shard, dense_shard, up_shard, down_shard, _, _, _, _, _, _, _, _, small = pl.pallas_call(
-        functools.partial(scatter_kernel, groups),
-        in_specs=[hbm] * 12 + [vmem] * 3,
-        out_specs=[hbm] * 14 + [vmem],
-        out_shape=[
-            shape((length, width), B),
-            shape((length, width), B),
-            shape((part, 6 * size), F),
-            shape(dense_weight.shape, F),
-            shape(up_weight.shape, F),
-            shape(down_weight.shape, F),
             shape((3, part, columns), B),
             shape((3, part, columns), B),
             shape((3, half_width, columns), B),
@@ -1865,28 +2054,24 @@
         ],
         scratch_shapes=[
             pltpu.VMEM((3, width, columns), B),
-            pltpu.VMEM((count, hidden), B),
-            pltpu.VMEM((count, hidden), B),
-            pltpu.VMEM((tall, width), B),
-            pltpu.VMEM((2, count, part), B),
-            pltpu.VMEM((2, CHUNK, hidden), F),
-            pltpu.VMEM((tall, 3 * size), B),
-            pltpu.VMEM((count, size), B),
-            pltpu.VMEM((2, half_width, columns), F),
-            pltpu.VMEM((half_width, columns), B),
-            pltpu.VMEM((2, half_width // 2, columns), B),
-            pltpu.VMEM((2, part, columns), B),
-            pltpu.VMEM((part, columns), B),
-            pltpu.VMEM((tall, width), B),
-            pltpu.VMEM((2, tall, CHUNK), B),
-            pltpu.VMEM((tall, CHUNK), F),
-            pltpu.VMEM((2, 2, quarter, width), B),
-            pltpu.VMEM((2, 2, quarter, width), F),
-            pltpu.VMEM((tall, 128), F),
-            pltpu.VMEM((tall, 128), F),
-            pltpu.VMEM((1, hidden), F),
-            pltpu.VMEM((8, width), F),
+            pltpu.VMEM((3, part, columns), B),
+            pltpu.VMEM((1, length), jnp.int32),
+            pltpu.VMEM((1, 3 * size), F),
+            pltpu.VMEM((1, width), F),
             pltpu.VMEM((5, 8, width), F),
+            dma((28,)),
+            dma((28,)),
+            dma((3, 6)),
+            dma((3,)),
+            dma((3,)),
+            dma((3, 3)),
+            dma((2, 2)),
+            dma((2, 3 + hidden // part)),
+            dma((2,)),
+            dma((2, 2)),
+            dma((2, 5)),
+            dma((2, 2)),
+            dma((5,)),
             dma((9,)),
             dma((5, 2)),
             dma((3, 4)),
@@ -1912,26 +2097,22 @@
             dma((5,)),
         ],
         compiler_params=pltpu.CompilerParams(
-            collective_id=1, has_side_effects=True, vmem_limit_bytes=67043328
+            collective_id=0, has_side_effects=True, vmem_limit_bytes=67043328
         ),
-        cost_estimate=pl.CostEstimate(flops=60 * 10**9, bytes_accessed=10**8, transcendentals=10**7),
-        name="scatter",
+        cost_estimate=pl.CostEstimate(flops=100 * 10**9, bytes_accessed=2 * 10**8, transcendentals=10**7),
+        name="layer",
     )(
-        attn_send,
-        attn_keep,
-        weights,
-        x_pair,
-        g_pair,
-        mlp_in,
-        mixed_grad,
-        context,
-        activation,
-        slope,
+        qkv_weight.reshape(part, 6 * size),
+        dense_weight,
+        up_weight,
+        down_weight,
+        segment_ids,
         own_x,
         own_g,
         vectors,
-        mixed_sum,
-        bias_sum,
+        up_here,
+        offsets,
+        jnp.stack(tables),
     )
 
     norms, bias_grad, up_bias_grad = small[0:4], small[4], small[5]

time: 398 us -> 382 us (0.960)
  Pallas kernels: 361 us -> 343 us
    pallas_call x2 -> x1, Pallas kernels: 361 us -> 343 us  [body(): pl.pallas_call(functools.partial(layer_kernel, groups, scoped_one, scoped...]
where the time goes in v1:
time: 382 us; the launch traced here: 376 us
  Pallas kernels  343 us (90%)
  local copies, waits for them, and re-layouts  27.5 us (7%)
  other arithmetic  4.3 us (1%)
    pallas_call x1, Pallas kernels, body(): pl.pallas_call(functools.partial(layer_kernel, groups, scoped_one, scoped...  343 us
    unnamed x21, local copies, waits for them, and re-layouts  17.1 us

profile of v1, /device:TPU:0, one launch (start us, length us, event | category | flops | bytes accessed | tf_op | source)
XLA Modules:
  0.0 375.8 jit_solution(14403206242072388164)
XLA Ops:
  0.7 0.7 constant_dynamic-slice_fusion.1
  1.4 0.1 pad.11.clone
  1.5 0.1 pad.14.clone
  1.5 0.8 constant_dynamic-slice_fusion
  2.3 0.6 copy.37
  2.9 1.3 dynamic_slice.9
  4.2 1.5 stack.48.vec_ref
  5.7 2.0 fusion.1
  7.7 0.5 maximum_bitcast_fusion.1
  8.2 0.0 copy-start.3
  8.2 1.2 pad_maximum_fusion.tables_ref
  9.4 0.7 copy-done.3
  10.1 1.1 copy.33
  11.2 1.6 copy.34.qkv_ref
  12.8 343.1 %layer.1 = (bf16[1024,2048]{1,0:T(8,128)(2,1)}, bf16[1024,2048]{1,0:T(8,128)(2,1)}, f32[256,1536]{1,0:T(8,128)}, f32[2,256,256]{2,1,0:T(8,128)}, f32[256,2048]{1...) custom-call(f32[256,1536]{1,0:T(8,128)} %copy.34.qkv_ref, ...), custom_call_target="tpu_custom_call" | custom-call | flops 99999997952 | bytes 200000000 | tf_op jit(solution)/shard_map/layer/pallas_call | solution.py:2022
  355.9 1.8 fusion.3
  357.7 0.0 copy-start.5
  357.8 0.6 slice.60
  358.3 0.6 pad_maximum_fusion.1
  358.9 1.9 copy.35
  360.8 2.1 copy.36
  362.9 0.0 copy-done.5
  362.9 0.6 copy.44
  363.5 4.9 %copy.45 = bf16[1,1024,2048]{2,1,0:T(8,128)(2,1)} copy(bf16[1,1024,2048]{2,1,0:T(8,128)(2,1)} %bitcast.34) | data formatting | bytes 8388608
  368.4 0.0 copy-done
  368.5 2.1 copy.46
  370.6 0.0 copy-done.4
  370.6 0.8 copy.47
  371.4 0.5 copy-done.2
  371.9 1.3 copy.48
  373.2 1.0 copy-done.1
  374.3 1.3 copy.49
  (14 shorter events, 0.1 us)
Async XLA Ops:
  8.2 2.0 copy-start.3
  357.7 5.2 %copy-start.5 = (f32[1,2048]{1,0:T(1,128)}, f32[1,2048]{1,0:T(1,128)S(1)}, u32[]{:S(2)}) copy-start(f32[1,2048]{1,0:T(1,128)S(1)} %get-tuple-element.62) | copy-start | bytes 24580
  363.5 4.9 %copy-start = (bf16[1024,2048]{1,0:T(8,128)(2,1)S(1)}, bf16[1024,2048]{1,0:T(8,128)(2,1)}, u32[]{:S(2)}) copy-start(bf16[1024,2048]{1,0:T(8,128)(2,1)} %get-tuple-element.23) | copy-start | bytes 12582916
  368.4 2.1 copy-start.4
  368.5 3.5 copy-start.2
  371.9 2.3 copy-start.1

commit v2 on v1

--- a/solution.py
+++ b/solution.py
@@ -115,6 +115,14 @@
 
 MESH = pl.DeviceIdType.MESH
 CHUNK = 256
+
+
+def by_rows(count, work, rows=64):
+    def one(number, carry):
+        work(pl.ds(pl.multiple_of(number * rows, rows), rows))
+        return carry
+
+    lax.fori_loop(0, count // rows, one, 0)
 
 
 def bit_of(index, bit):
@@ -294,7 +302,8 @@
     g_ref,
     vec_ref,
     up_bias_ref,
-    offset_ref,
+    qv_ref,
+    key_ref,
     tables_ref,
     w_relay,
     x_other,
@@ -535,15 +544,20 @@
         def work(tile, slot):
             here = pl.ds(pl.multiple_of(tile * CHUNK, CHUNK), CHUNK)
             both = pl.ds(pl.multiple_of(seq * length + tile * CHUNK, CHUNK), CHUNK)
-            mean, inverse = stats(raw_x[slot].astype(F))
-            for position, mask in enumerate(order):
-                to = slice(position * part, (position + 1) * part)
-                there = pl.ds(pl.multiple_of(flip(me, mask) * part, part), part)
-                piece = raw_x[slot, :, there]
-                normed = (piece.astype(F) - mean) * inverse
-                attn_v[here, to] = (normed * vec_ref[0:1, there] + vec_ref[1:2, there]).astype(B)
-                mlp_v[both, to] = (normed * vec_ref[2:3, there] + vec_ref[3:4, there]).astype(B)
-                xr_v[here, to] = piece
+            raw, attn_to, mlp_to, x_to = raw_x.at[slot], attn_v.at[here], mlp_v.at[both], xr_v.at[here]
+
+            def some(at):
+                mean, inverse = stats(raw[at].astype(F))
+                for position, mask in enumerate(order):
+                    to = slice(position * part, (position + 1) * part)
+                    there = pl.ds(pl.multiple_of(flip(me, mask) * part, part), part)
+                    piece = raw[at, there]
+                    normed = (piece.astype(F) - mean) * inverse
+                    attn_to[at, to] = (normed * vec_ref[0:1, there] + vec_ref[1:2, there]).astype(B)
+                    mlp_to[at, to] = (normed * vec_ref[2:3, there] + vec_ref[3:4, there]).astype(B)
+                    x_to[at, to] = piece
+
+            by_rows(CHUNK, some)
 
         over_tiles(x_other if seq else x_ref, raw_x, 0, work)
         both = pl.ds(seq * length, length)
@@ -559,12 +573,17 @@
 
         def work(tile, slot):
             here = pl.ds(pl.multiple_of(tile * CHUNK, CHUNK), CHUNK)
-            if seq == 0:
-                bias_ref[...] += jnp.sum(raw_x[slot].astype(F), axis=0, keepdims=True)
-            for position, mask in enumerate(order):
-                to = slice(position * part, (position + 1) * part)
-                there = pl.ds(pl.multiple_of(flip(me, mask) * part, part), part)
-                g_v[here, to] = raw_x[slot, :, there]
+            raw, g_to = raw_x.at[slot], g_v.at[here]
+
+            def some(at):
+                if seq == 0:
+                    bias_ref[...] += jnp.sum(raw[at].astype(F), axis=0, keepdims=True)
+                for position, mask in enumerate(order):
+                    to = slice(position * part, (position + 1) * part)
+                    there = pl.ds(pl.multiple_of(flip(me, mask) * part, part), part)
+                    g_to[at, to] = raw[at, there]
+
+            by_rows(CHUNK, some, 32)
 
         over_tiles(g_other if seq else g_ref, raw_x, 1, work)
         leave(("g", seq), g_v, g_rel.at[pl.ds(seq * length, length)], rel_sem.at[seq, 1])
@@ -577,23 +596,29 @@
 
     def project(seq):
         whole_group(0)
+        key_row = jnp.concatenate([key_ref[pl.ds(half, 1)], jnp.zeros((1, size - ROT), F)], axis=1)
+        offsets = (qv_ref[half, 0:1], key_row, qv_ref[half, 1:2])
         if seq == 0:
             left("tables")
 
         def one(tile, carry):
             here = pl.ds(pl.multiple_of(tile * CHUNK, CHUNK), CHUNK)
-            mixed = dot(attn_v[here], w[0, :, : 3 * size], ((1,), (0,)), F) + offset_ref[...]
+            mixed = dot(attn_v[here], w[0, :, : 3 * size], ((1,), (0,)), F)
             tables = (tab_v[0, here], tab_v[1, here], tab_v[2, here])
-            q_v[here] = turn(mixed[:, :size], *tables).astype(B)
-            k_v[here] = turn(mixed[:, size : 2 * size], *tables).astype(B)
-            v_v[here] = mixed[:, 2 * size :].astype(B)
+            q_v[here] = turn(mixed[:, :size] + offsets[0], *tables).astype(B)
+            k_v[here] = turn(mixed[:, size : 2 * size] + offsets[1], *tables).astype(B)
+            v_v[here] = (mixed[:, 2 * size :] + offsets[2]).astype(B)
             return carry
 
         lax.fori_loop(0, length // CHUNK, one, 0)
 
     def project_grad(seq):
         whole_group(0)
-        cg_v[...] = dot(g_v[...], w[0, :, 3 * size :], ((1,), (0,)), B)
+
+        def some(at):
+            cg_v[at] = dot(g_v[at], w[0, :, 3 * size :], ((1,), (0,)), B)
+
+        by_rows(length, some, CHUNK)
 
     def attend(seq):
         if seq:
@@ -602,14 +627,17 @@
         scale = size ** (-0.5)
         ids = seg_ref[...] if seq == 0 else seg_v[...]
         col_v[...] = jnp.broadcast_to(ids.astype(F), (8, length)).T
-        dk_v[...] = jnp.zeros_like(dk_v)
-        dv_v[...] = jnp.zeros_like(dv_v)
-        for first in range(0, length, QBLOCK):
-            low, high = key_range(first)
-            here, keys = slice(first, first + QBLOCK), slice(low, high)
+
+        def clear(here):
+            dk_v[here] = jnp.zeros((128, size), F)
+            dv_v[here] = jnp.zeros((128, size), F)
+
+        by_rows(length, clear, 128)
+        def queries(first, low, reach):
+            here, keys = pl.ds(first, QBLOCK), pl.ds(low, reach)
             scores = dot(q_v[here], k_v[keys], ((1,), (1,)), F) * scale
-            row_ids = first + lax.broadcasted_iota(jnp.int32, (QBLOCK, high - low), 0)
-            key_ids = low + lax.broadcasted_iota(jnp.int32, (QBLOCK, high - low), 1)
+            row_ids = first + lax.broadcasted_iota(jnp.int32, (QBLOCK, reach), 0)
+            key_ids = low + lax.broadcasted_iota(jnp.int32, (QBLOCK, reach), 1)
             row = seg_ref[:, keys] if seq == 0 else seg_v[:, keys]
             allowed = (key_ids <= row_ids) & (col_v[here, 0:1] == row.astype(F))
             scores = jnp.where(allowed, scores, -1e30)
@@ -625,16 +653,30 @@
             tables = (tab_v[0, here], -tab_v[1, here], -tab_v[2, here])
             mg_v[here, :size] = turn(q_grad, *tables).astype(B)
             dk_v[keys] += dot(score_grad, q_v[here], ((0,), (0,)), F) * scale
-        for first in range(0, length, QBLOCK):
-            here = slice(first, first + QBLOCK)
+
+        for first in range(0, DOC_MAX, QBLOCK):
+            queries(first, 0, first + QBLOCK)
+
+        def later(number, carry):
+            low = pl.multiple_of(number * QBLOCK - DOC_MAX, QBLOCK)
+            queries(pl.multiple_of(number * QBLOCK, QBLOCK), low, DOC_MAX + QBLOCK)
+            return carry
+
+        lax.fori_loop(DOC_MAX // QBLOCK, length // QBLOCK, later, 0)
+
+        def turn_back(here):
             tables = (tab_v[0, here], -tab_v[1, here], -tab_v[2, here])
             mg_v[here, size : 2 * size] = turn(dk_v[here], *tables).astype(B)
             mg_v[here, 2 * size :] = dv_v[here].astype(B)
-        sums = jnp.sum(mg_v[...].astype(F), axis=0, keepdims=True)
+
+        by_rows(length, turn_back)
         if seq == 0:
-            sum_ref[...] = sums
-        else:
-            sum_ref[...] += sums
+            sum_ref[...] = jnp.zeros_like(sum_ref)
+
+        def add_sums(here):
+            sum_ref[...] += jnp.sum(mg_v[here].astype(F), axis=0, keepdims=True)
+
+        by_rows(length, add_sums, 128)
         both = pl.ds(seq * length, length)
         leave(("mg", seq), mg_v, mixed_out.at[both], rel_sem.at[seq, 3])
         leave(("ctx", seq), ctx_v, ctx_out.at[both], rel_sem.at[seq, 4])
@@ -665,17 +707,24 @@
         def one(tile, carry):
             slot = lax.rem(tile, 2)
             here = pl.ds(pl.multiple_of(tile * CHUNK, CHUNK), CHUNK)
-            pre = dot(mlp_v[here], w[1], ((1,), (0,)), F) + up_bias_ref[...]
+            pre = dot(mlp_v[here], w[1], ((1,), (0,)), F) + up_bias_ref[:, pl.ds(pl.multiple_of(half * hidden, hidden), hidden)]
 
             @pl.when(tile >= low + 2)
             def _():
                 for copy in store(tile - 2, slot):
                     copy.wait()
 
-            cumulative = 0.5 * (1.0 + lax.erf(pre * 0.7071067811865476))
-            density = jnp.exp(-0.5 * pre * pre) * 0.3989422804014327
-            act_v[slot] = (pre * cumulative).astype(B)
-            slope_v[slot] = cumulative + pre * density
+            slope_v[slot] = pre
+            act_to, slope_to = act_v.at[slot], slope_v.at[slot]
+
+            def some(at):
+                pre = slope_to[at]
+                cumulative = 0.5 * (1.0 + lax.erf(pre * 0.7071067811865476))
+                density = jnp.exp(-0.5 * pre * pre) * 0.3989422804014327
+                act_to[at] = (pre * cumulative).astype(B)
+                slope_to[at] = cumulative + pre * density
+
+            by_rows(CHUNK, some)
             for copy in store(tile, slot):
                 copy.start()
             return carry
@@ -710,7 +759,10 @@
         if seq and number:
             leave("keep", grad_v.at[pl.ds(0, middle)], keep_out, out_sem.at[4])
         elif seq:
-            send_v[...] = grad_v[middle:].astype(B)
+            def narrow(at):
+                send_v[at] = grad_v.at[pl.ds(middle, middle)][at].astype(B)
+
+            by_rows(middle, narrow, 128)
             leave("send", send_v, send_out, out_sem.at[3])
 
     def lift(seq):
@@ -1012,7 +1064,14 @@
         )[group]
         p_copy(group).wait_recv()
         staged(far_in.at[group])
-        block[...] = y_stage[...].astype(F)
+
+        def widen(at):
+            block[at] = y_stage[at].astype(F)
+
+        def add(at):
+            block[at] += y_stage[at].astype(F)
+
+        by_rows(part, widen)
 
         @pl.when(inner)
         def _():
@@ -1020,7 +1079,7 @@
                 p_send.at[0], far_two.at[group], two_sem.at[group], two_sem.at[group], "dp", across_to
             ).wait_recv()
             staged(far_two.at[group])
-            block[...] += y_stage[...].astype(F)
+            by_rows(part, add)
 
         emit(group, 1, block, 1 - half)
 
@@ -1034,11 +1093,15 @@
             need(5)
         y_copy(group, position).wait_recv()
         staged(y_recv.at[group, span(position)])
-        total = keep_v[slot_of[group], span(position)] + y_stage[...].astype(F)
         onward, aside = z_copy(group, position)
         if group == 1:
             z_copy(0, position)[0].wait_send()
-        z_send[slot_of[group], span(position - 2)] = total.astype(B)
+        kept, target = keep_v.at[slot_of[group], span(position)], z_send.at[slot_of[group], span(position - 2)]
+
+        def add(at):
+            target[at] = (kept[at] + y_stage[at].astype(F)).astype(B)
+
+        by_rows(part, add)
         pl.when(inner)(onward.start)
         pl.when(outer)(aside.start)
 
@@ -1047,32 +1110,44 @@
             need(5)
         y_copy(group, position).wait_recv()
         staged(y_recv.at[group, span(position)])
-        total = keep_v[slot_of[group], span(position)] + y_stage[...].astype(F)
-        keep_v[slot_of[group], span(position)] = total
+        kept, target = keep_v.at[slot_of[group], span(position)], p_send.at[slot_of[group]]
+        if position == 1 and group == 1:
+            p_copy(0).wait_send()
+
+        def add(at):
+            total = kept[at] + y_stage[at].astype(F)
+            kept[at] = total
+            if position == 1:
+                target[at] = total.astype(B)
+
+        by_rows(part, add)
         if position == 1:
-            if group == 1:
-                p_copy(0).wait_send()
-
-            @pl.when(outer)
-            def _():
-                p_send[slot_of[group]] = keep_v[slot_of[group], span(1)].astype(B)
-                p_copy(group).start()
+            pl.when(outer)(p_copy(group).start)
 
     def z_last(group, position):
-        def add():
+        kept, target = keep_v.at[slot_of[group], span(position)], p_send.at[slot_of[group]]
+
+        def add(at):
+            total = kept[at] + y_stage[at].astype(F)
+            if position == 1:
+                target[at] = total.astype(B)
+            else:
+                kept[at] = total
+
+        def add_all():
             z_arrived(group, position).wait_recv()
             staged(z_recv.at[group, span(position)])
-            return keep_v[slot_of[group], span(position)] + y_stage[...].astype(F)
+            by_rows(part, add)
 
         if position == 1:
 
             @pl.when(inner)
             def _():
-                p_send[slot_of[group]] = add().astype(B)
+                add_all()
                 p_copy(group).start()
 
         else:
-            keep_v[slot_of[group], span(0)] = add()
+            add_all()
             emit_near(group)
 
     loads = [
@@ -1363,30 +1438,32 @@
         for copy in copies:
             copy.wait()
         here = pl.ds(which * quarter, quarter)
-        if which == 0:
-            total_u, total_un = 0.0, 0.0
-            mean, inverse = stats(tile_v[quarter:].astype(F))
+        held, sent, own_x, g_rows = hold_v.at[which, 0], tile_v, tile_v.at[pl.ds(quarter, quarter)], x_send.at[0, 0]
+        target = c_send.at[here]
+
+        def total(at, block):
+            mine = held[at, step(position_of(block), part)]
+            return mine + sent[at, step(position_of(block, True), part)].astype(F)
+
+        def some_grad(at):
+            rows = own_x[at].astype(F)
+            mean, inverse = stats(rows)
+            normed = (rows - mean) * inverse
+            blend = jnp.concatenate([total(at, block) for block in range(groups)], axis=1)
+            inner_grad = (
+                blend
+                - jnp.mean(blend, axis=1, keepdims=True)
+                - normed * jnp.mean(blend * normed, axis=1, keepdims=True)
+            )
+            target[at] = (g_rows[at].astype(F) + inner_grad * inverse).astype(B)
+
+        def some_out(at):
             for block in range(groups):
-                mine = hold_v[0, 0, :, step(position_of(block), part)]
-                theirs = tile_v[0:quarter, step(position_of(block, True), part)].astype(F)
-                blend = mine + theirs
-                normed = (tile_v[quarter:, block * part : (block + 1) * part].astype(F) - mean) * inverse
-                hold_v[0, 1, :, block * part : (block + 1) * part] = blend
-                total_u = total_u + jnp.sum(blend, axis=1, keepdims=True)
-                total_un = total_un + jnp.sum(blend * normed, axis=1, keepdims=True)
-            mean_u, mean_un = total_u * (1.0 / width), total_un * (1.0 / width)
-            for block in range(groups):
-                at = slice(block * part, (block + 1) * part)
-                normed = (tile_v[quarter:, at].astype(F) - mean) * inverse
-                inner = (hold_v[0, 1, :, at] - mean_u - normed * mean_un) * inverse
-                c_send[here, at] = (x_send[0, 0, :, at].astype(F) + inner).astype(B)
-        else:
-            for block in range(groups):
-                at = slice(block * part, (block + 1) * part)
-                mine = hold_v[1, 0, :, step(position_of(block), part)]
-                theirs = tile_v[0:quarter, step(position_of(block, True), part)].astype(F)
-                bias = vec_ref[4:5, at] + vec_ref[5:6, at]
-                c_send[here, at] = (tile_v[quarter:, at].astype(F) + (mine + theirs) + bias).astype(B)
+                cut = slice(block * part, (block + 1) * part)
+                bias = vec_ref[4:5, cut] + vec_ref[5:6, cut]
+                target[at, cut] = (own_x[at, cut].astype(F) + total(at, block) + bias).astype(B)
+
+        by_rows(quarter, some_out if which else some_grad)
         first = remote(
             c_send.at[here], out_ref.at[spot(core, side)], fs_sem.at[which, 0], fr_sem.at[which, 0], "tensor", side_to
         )
@@ -1489,7 +1566,8 @@
     g_ref,
     vec_ref,
     up_bias_ref,
-    offset_ref,
+    qv_ref,
+    key_ref,
     tables_ref,
     block_out,
     input_grad,
@@ -1572,7 +1650,8 @@
         g_ref,
         vec_ref,
         up_bias_ref,
-        offset_ref,
+        qv_ref,
+        key_ref,
         tables_ref,
         w_relay,
         x_other,
@@ -1964,11 +2043,7 @@
     vectors = jnp.stack([attn_norm_gain, attn_norm_bias, mlp_norm_gain, mlp_norm_bias, dense_bias, down_bias])
     own_x, own_g = tokens[0], out_grad[0]
 
-    qv_here, key_here = pick(qv_bias, half, 0), pick(key_bias, half, 0)
-    key_full = jnp.concatenate([key_here, jnp.zeros((heads, size - ROT), F)], axis=1)
-    offsets = jnp.stack([qv_here[:, 0], key_full, qv_here[:, 1]], axis=1).reshape(1, 3 * size)
     tables = rope_tables(length)
-    up_here = pick(up_bias, half, 0)[None]
     columns = hidden
     half_width = width // 2
     vmem, hbm = pl.BlockSpec(memory_space=pltpu.VMEM), pl.BlockSpec(memory_space=pl.ANY)
@@ -2021,7 +2096,7 @@
     ]
     block_out, input_grad, qkv_shard, dense_shard, up_shard, down_shard, *_, small = pl.pallas_call(
         functools.partial(layer_kernel, groups, scoped_one, scoped_two),
-        in_specs=[hbm] * 4 + [vmem] + [hbm] * 2 + [vmem] * 3 + [hbm],
+        in_specs=[hbm] * 4 + [vmem] + [hbm] * 2 + [vmem] * 4 + [hbm],
         out_specs=[hbm] * 26 + [vmem],
         out_shape=[
             shape((length, width), B),
@@ -2110,8 +2185,9 @@
         own_x,
         own_g,
         vectors,
-        up_here,
-        offsets,
+        up_bias.reshape(1, 2 * hidden),
+        qv_bias,
+        key_bias,
         jnp.stack(tables),
     )
 

time: 382 us -> 376 us (0.984)
    unnamed x21 -> x20, local copies, waits for them, and re-layouts: 17.1 us -> 16.4 us
where the time goes in v2:
time: 376 us; the launch traced here: 373 us
  Pallas kernels  344 us (91%)
  local copies, waits for them, and re-layouts  24 us (6%)
  other arithmetic  4.29 us (1%)
    pallas_call x1, Pallas kernels, body(): pl.pallas_call(functools.partial(layer_kernel, groups, scoped_one, scoped...  344 us
    unnamed x20, local copies, waits for them, and re-layouts  16.4 us

profile of v2, /device:TPU:0, one launch (start us, length us, event | category | flops | bytes accessed | tf_op | source)
XLA Modules:
  0.0 373.3 jit_solution(8129664121323894214)
XLA Ops:
  0.7 0.1 pad.13.clone
  0.7 0.1 pad.10.clone
  0.8 1.5 stack.42.vec_ref
  2.3 2.0 fusion.1
  4.3 0.5 maximum_bitcast_fusion.1
  4.8 0.0 copy-start.3
  4.8 1.2 pad_maximum_fusion.tables_ref
  6.0 0.7 copy-done.3
  6.8 0.9 copy.33
  7.7 1.6 copy.34.qkv_ref
  9.3 344.3 %layer.1 = (bf16[1024,2048]{1,0:T(8,128)(2,1)}, bf16[1024,2048]{1,0:T(8,128)(2,1)}, f32[256,1536]{1,0:T(8,128)}, f32[2,256,256]{2,1,0:T(8,128)}, f32[256,2048]{1...) custom-call(f32[256,1536]{1,0:T(8,128)} %copy.34.qkv_ref, ...), custom_call_target="tpu_custom_call" | custom-call | flops 99999997952 | bytes 200000000 | tf_op jit(solution)/shard_map/layer/pallas_call | solution.py:2097
  353.6 1.8 fusion.3
  355.5 0.0 copy-start.5
  355.5 0.6 slice.52
  356.1 0.6 pad_maximum_fusion.1
  356.7 1.9 copy.35
  358.6 2.1 copy.36
  360.6 0.0 copy-done.5
  360.6 0.6 copy.43
  361.2 0.0 copy-start
  361.2 4.9 %copy.44 = bf16[1,1024,2048]{2,1,0:T(8,128)(2,1)} copy(bf16[1,1024,2048]{2,1,0:T(8,128)(2,1)} %bitcast.29) | data formatting | bytes 8388608
  366.2 0.0 copy-done
  366.2 0.0 copy-start.4
  366.2 0.0 copy-start.2
  366.2 2.1 copy.45
  368.3 0.0 copy-done.4
  368.3 0.8 copy.46
  369.1 0.5 copy-done.2
  369.7 0.0 copy-start.1
  369.7 1.3 copy.47
  371.0 1.0 copy-done.1
  372.0 1.3 copy.48
  (8 shorter events, 0.1 us)
Async XLA Ops:
  4.8 2.0 copy-start.3
  355.5 5.2 %copy-start.5 = (f32[1,2048]{1,0:T(1,128)}, f32[1,2048]{1,0:T(1,128)S(1)}, u32[]{:S(2)}) copy-start(f32[1,2048]{1,0:T(1,128)S(1)} %get-tuple-element.62) | copy-start | bytes 24580
  361.2 4.9 %copy-start = (bf16[1024,2048]{1,0:T(8,128)(2,1)S(1)}, bf16[1024,2048]{1,0:T(8,128)(2,1)}, u32[]{:S(2)}) copy-start(bf16[1024,2048]{1,0:T(8,128)(2,1)} %get-tuple-element.23) | copy-start | bytes 12582916
  366.2 2.1 copy-start.4
  366.2 3.5 copy-start.2
  369.7 2.3 copy-start.1

commit v3 on v2

--- a/solution.py
+++ b/solution.py
@@ -1757,6 +1757,30 @@
 
     pl.run_scoped(first, *scoped_one)
     pl.run_scoped(second, *scoped_two)
+
+
+def place_kernel(*refs):
+    count = (len(refs) - 2) // 3
+    sources, targets, staging = refs[:count], refs[count : 2 * count], refs[2 * count : 3 * count]
+    in_sem, out_sem = refs[3 * count :]
+    pieces = []
+    for number, (source, target, stage) in enumerate(zip(sources, targets, staging)):
+        rows = source.shape[0] // 2
+        for part in range(2):
+            at = pl.ds(part * rows, rows)
+            pieces.append(
+                (
+                    pltpu.make_async_copy(source.at[at], stage.at[at], in_sem.at[number, part]),
+                    pltpu.make_async_copy(stage.at[at], target.at[at], out_sem.at[number, part]),
+                )
+            )
+    for load, _ in pieces:
+        load.start()
+    for load, store in pieces:
+        load.wait()
+        store.start()
+    for _, store in pieces:
+        store.wait()
 
 
 def body_narrow(
@@ -2191,6 +2215,17 @@
         jnp.stack(tables),
     )
 
+    made = [block_out, input_grad, dense_shard, up_shard, down_shard]
+    block_out, input_grad, dense_shard, up_shard, down_shard = pl.pallas_call(
+        place_kernel,
+        in_specs=[hbm] * len(made),
+        out_specs=[hbm] * len(made),
+        out_shape=[shape(a.shape, a.dtype) for a in made],
+        scratch_shapes=[pltpu.VMEM(a.shape, a.dtype) for a in made] + [dma((len(made), 2)), dma((len(made), 2))],
+        compiler_params=pltpu.CompilerParams(vmem_limit_bytes=67043328),
+        cost_estimate=pl.CostEstimate(flops=0, bytes_accessed=28 * 10**6, transcendentals=0),
+        name="place",
+    )(*made)
     norms, bias_grad, up_bias_grad = small[0:4], small[4], small[5]
     mixed_bias = small[6].reshape(2, width // 2)[:, : 3 * size].reshape(2, 3, size)
     qv_grad = jnp.stack([mixed_bias[:, 0], mixed_bias[:, 2]], axis=1)

time: 376 us -> 373 us (level)
  local copies, waits for them, and re-layouts: 24 us -> 11.9 us
  Pallas kernels: 344 us -> 354 us
    unnamed x20 -> x7, local copies, waits for them, and re-layouts: 16.4 us -> 4.33 us
    pallas_call x0 -> x1, Pallas kernels: none -> 9.2 us  [body(): pl.pallas_call(place_kernel, in_specs=[hbm] * len(made), out_specs=[hbm]...]
where the time goes in v3:
time: 373 us; the launch traced here: 370 us
  Pallas kernels  354 us (95%)
  local copies, waits for them, and re-layouts  11.9 us (3%)
  other arithmetic  4.29 us (1%)
    pallas_call x1, Pallas kernels, body(): pl.pallas_call(functools.partial(layer_kernel, groups, scoped_one, scoped...  344 us
    pallas_call x1, Pallas kernels, body(): pl.pallas_call(place_kernel, in_specs=[hbm] * len(made), out_specs=[hbm]...  9.2 us

profile of v3, /device:TPU:0, one launch (start us, length us, event | category | flops | bytes accessed | tf_op | source)
XLA Modules:
  0.0 370.4 jit_solution(5480389738096607960)
XLA Ops:
  0.7 0.1 pad.13.clone
  0.7 0.1 pad.10.clone
  0.8 1.5 stack.42.vec_ref
  2.3 2.0 fusion.1
  4.3 0.5 maximum_bitcast_fusion.1
  4.8 0.0 copy-start
  4.8 1.2 pad_maximum_fusion.tables_ref
  6.0 0.7 copy-done
  6.8 0.9 copy.33
  7.7 1.6 copy.34.qkv_ref
  9.3 344.3 %layer.1 = (bf16[1024,2048]{1,0:T(8,128)(2,1)}, bf16[1024,2048]{1,0:T(8,128)(2,1)}, f32[256,1536]{1,0:T(8,128)}, f32[2,256,256]{2,1,0:T(8,128)}, f32[256,2048]{1...) custom-call(f32[256,1536]{1,0:T(8,128)} %copy.34.qkv_ref, ...), custom_call_target="tpu_custom_call" | custom-call | flops 99999997952 | bytes 200000000 | tf_op jit(solution)/shard_map/layer/pallas_call | solution.py:2121
  353.6 9.2 %place.1 = (bf16[1024,2048]{1,0:T(8,128)(2,1)}, bf16[1024,2048]{1,0:T(8,128)(2,1)}, f32[2,256,256]{2,1,0:T(8,128)}, f32[256,2048]{1,0:T(8,128)}, f32[2048,256]{1,0:T(8,128)}) custom-call(bf16[1024,2048]{1,0:T(8,128)(2,1)} %get-tuple-element.27.refs_0_, bf16[1024,2048]{1,0:T(8,128)(2,1)} %get-tuple-element.28.refs_1_, ...), custom_call_target="tpu_custom_call" | custom-call | bytes 28000000 | tf_op jit(solution)/shard_map/place/pallas_call | solution.py:2219
  362.8 1.8 fusion.3
  364.7 0.0 copy-start.1
  364.7 0.6 slice.52
  365.3 0.6 pad_maximum_fusion.1
  365.9 1.9 copy.35
  367.7 2.1 copy.36
  369.8 0.0 copy-done.1
  369.8 0.6 copy.38
  (8 shorter events, 0.1 us)
Async XLA Ops:
  4.8 2.0 copy-start
  364.7 5.2 %copy-start.1 = (f32[1,2048]{1,0:T(1,128)}, f32[1,2048]{1,0:T(1,128)S(1)}, u32[]{:S(2)}) copy-start(f32[1,2048]{1,0:T(1,128)S(1)} %get-tuple-element.72) | copy-start | bytes 24580
